TPU v7x, 256 devices: a whole 4x4x8 slice. The times are simulated.
256 devices in a mesh: stn: 16 (over z, core), seg: 16 (over x, y).
Axes of the slice: x: 4, y: 4, z: 8, core: 2. Of those that a mesh axis runs over, the one named last changes fastest.
Arguments:
- voltages: bfloat16 [128, 32, 32768], P('stn', None, 'seg'), may hold values from -91 to 91
- filter_taps: float32 [8, 32], replicated, may hold values from -0.375 to 0.375
- positions: float32 [2, 128], replicated, may hold values from -8 to 8
- beam_dirs: int32 [128], replicated, may hold values from 0 to 359
- chan_table: int32 [16], replicated, may hold values from 0 to 15, each once
Outputs:
- beam_out: bfloat16 [16, 2, 128, 32768], P('stn', None, None, 'seg')
All inputs are finite; a program needn't handle non-finite values.
Results may differ from a plain program's by a relative error of at most 0.0078.
Values may be sent and summed in bfloat16 or wider, within the bound.
A program may use at most 64 MiB of HBM per device.

v0:
```python
import math

import jax
import jax.numpy as jnp
from jax import lax
from jax.sharding import PartitionSpec as P

C = 16
TAPS = 8
B = 128
DIRS = 360


loading_level = 0.1
full_turn = 2.0 * math.pi


def passed_along(value, axis, by):
    length = lax.axis_size(axis)
    pairs = [(i, i + by) for i in range(length) if 0 <= i + by < length]
    return lax.ppermute(value, axis, pairs)


def dft_tables(chan_table):
    frame_width = 2 * C
    phase_index = jnp.remainder(
        chan_table[:, None] * jnp.arange(frame_width, dtype=jnp.int32)[None, :], frame_width
    )
    angles = phase_index.astype(jnp.float32) * (full_turn / frame_width)
    return jnp.stack([jnp.cos(angles), -jnp.sin(angles)], axis=1)


def filter_block(station_block, filter_taps):
    snap_count = station_block.shape[2] - (TAPS - 1)
    widened = station_block.astype(jnp.float32)
    summed = jnp.zeros((station_block.shape[0], station_block.shape[1], snap_count), jnp.float32)
    for tap_index in range(TAPS):
        offset = TAPS - 1 - tap_index
        summed = (
            summed
            + filter_taps[tap_index][None, :, None] * widened[:, :, offset : offset + snap_count]
        )
    return summed


def channelize(filtered, dft_table):
    return jnp.einsum("jap,spt->jast", dft_table, filtered, precision=lax.Precision.HIGHEST).astype(
        jnp.bfloat16
    )


def halves(gram_full):
    half_size = gram_full.shape[-1] // 2
    sym_part = gram_full[..., :half_size, :half_size] + gram_full[..., half_size:, half_size:]
    skew_part = gram_full[..., half_size:, :half_size] - gram_full[..., :half_size, half_size:]
    return (sym_part, skew_part)


def assemble(sym_part, skew_part):
    upper_rows = jnp.concatenate([sym_part, -skew_part], axis=-1)
    bottom = jnp.concatenate([skew_part, sym_part], axis=-1)
    return jnp.concatenate([upper_rows, bottom], axis=-2)


def steering(positions, beam_dirs, channel):
    bearing = beam_dirs.astype(jnp.float32) * (full_turn / DIRS)
    frequency = 1.0 + channel.astype(jnp.float32) / C
    path_delay = (
        positions[0][:, None] * jnp.cos(bearing)[None, :]
        + positions[1][:, None] * jnp.sin(bearing)[None, :]
    )
    phases = full_turn * frequency * path_delay
    return jnp.concatenate([jnp.cos(phases), jnp.sin(phases)], axis=0)


def solve_weights(factor, steer):
    whitened = jax.scipy.linalg.solve_triangular(factor, steer, lower=True)
    column_power = jnp.sum(whitened * whitened, axis=0)
    solved = jax.scipy.linalg.solve_triangular(factor, whitened, lower=True, trans=1)
    return (solved / jnp.sqrt(column_power)[None, :]).astype(jnp.bfloat16)


def mixing(weights):
    half_size = weights.shape[0] // 2
    swapped = jnp.concatenate([-weights[half_size:], weights[:half_size]], axis=0)
    return jnp.concatenate([weights.T, swapped.T], axis=0)


def solve_slots(factor, positions, slot_dirs, channels):
    return jax.vmap(
        lambda one_factor, channel: solve_weights(
            one_factor, steering(positions, slot_dirs, channel)
        )
    )(factor, channels)


def on_device(voltages, filter_taps, positions, beam_dirs, chan_table):
    last_frames = voltages[:, :, voltages.shape[2] - (TAPS - 1) :]
    earlier = passed_along(last_frames, "seg", 1)
    extended = jnp.concatenate([earlier, voltages], axis=2)
    filtered = filter_block(extended, filter_taps)
    spectra = channelize(filtered, dft_tables(chan_table))
    turned = lax.all_to_all(spectra, "stn", split_axis=0, concat_axis=2, tiled=True)
    slot_count = turned.shape[0]
    snap_count = turned.shape[3]
    stacked = turned.reshape(slot_count, 2 * turned.shape[2], snap_count)
    gram_full = jnp.einsum("cat,cbt->cab", stacked, stacked, preferred_element_type=jnp.float32)
    sym_part, skew_part = halves(gram_full)
    segments = lax.axis_size("seg")
    snap_total = snap_count * segments
    identity = jnp.eye(stacked.shape[1], dtype=jnp.float32)
    sym_part, skew_part = lax.psum((sym_part, skew_part), "seg")
    covariance = assemble(sym_part, skew_part) / snap_total + loading_level * identity
    factor = jnp.linalg.cholesky(covariance)
    channels = lax.dynamic_slice_in_dim(chan_table, lax.axis_index("stn") * slot_count, slot_count)
    weights = solve_slots(factor, positions, beam_dirs, channels)
    mix_matrix = jax.vmap(mixing)(weights)
    beam_out = jnp.einsum("cbk,ckt->cbt", mix_matrix, stacked, preferred_element_type=jnp.float32)
    return beam_out.astype(jnp.bfloat16).reshape(slot_count, 2, B, snap_count)


def solution(mesh):
    return jax.shard_map(
        on_device,
        mesh=mesh,
        in_specs=(P("stn", None, "seg"), P(), P(), P(), P()),
        out_specs=P("stn", None, None, "seg"),
        check_vma=False,
    )
```

profile of v0, /device:TPU:1, one launch (start us, length us, event | category | flops | bytes accessed | tf_op | source)
XLA Modules:
  0.0 224.0 jit_solution(4464801377694888693)
XLA Ops:
  6.5 0.9 slice.142
  7.5 4.0 %collective-permute-start = (bf16[8,32,7]{2,1,0:T(8,128)(2,1)S(1)}, bf16[8,32,7]{2,1,0:T(8,128)(2,1)S(1)}, u32[]{:S(2)}, u32[]{:S(2)}) collective-permute-start(bf16[8,32,7]{2,1,0:T(8,128)(2,1)S(1)} %slice.142), channel_id=1, source_target_pairs={{0,1},{1,2},{2,3},{3,4},{4,5},{5,6},{6,7},{7,8},{8,9},{9,10},{10,1... | collective-permute-start | bytes 10760 | tf_op jit(solution)/shard_map/ppermute | solution.py:21
  11.5 0.8 fusion.54
  12.3 1.0 slice_bitcast_fusion.20
  13.3 1.6 maximum_convert_fusion
  14.9 5.8 %convolution_convert_fusion = bf16[16,2,8,2048]{3,0,2,1:T(8,128)(2,1)S(1)} fusion(f32[8,32,2055]{2,1,0:T(8,128)S(1)} %maximum_convert_fusion, f32[32]{0:T(128)S(1)} %get-tuple-element.53, f32[32]{0:T(128)S(1)} %get-tuple-element.54, f32[32]{0:T(128)S(1)} %get-tuple-element.48, f32[32]{0:T(128)S(1)} %get-tuple-element.49, f32[32]{0:T(128)S(1)} %get-tuple-element.50, ...), kind=kOutput, calls=%fused_computation.3 | convolution fusion | flops 209716224 | bytes 17846272 | tf_op jit(solution)/shard_map/jap,spt->jast/dot_general | solution.py:47
  20.7 1.5 copy.27
  22.3 9.5 %all-to-all-start = ((bf16[16,2,8,2048]{3,2,1,0:T(8,128)(2,1)}), bf16[16,2,8,2048]{3,2,1,0:T(8,128)(2,1)S(1)}, u32[]{:S(2)}, u32[]{:S(2)}) async-start(bf16[16,2,8,2048]{3,2,1,0:T(8,128)(2,1)} %copy.27), calls=%async_computation | async-start | bytes 2097152 | tf_op jit(solution)/shard_map/all_to_all | solution.py:103
  31.8 0.2 all-reduce.4.cloned.1.call-start
  32.1 27.7 %all-to-all-done = bf16[16,2,8,2048]{3,2,1,0:T(8,128)(2,1)S(1)} async-done(((bf16[16,2,8,2048]{3,2,1,0:T(8,128)(2,1)}), bf16[16,2,8,2048]{3,2,1,0:T(8,128)(2,1)S(1)}, u32[]{:S(2)}, u32[]{:S(2)}) %all-to-all-start) | async-done | bytes 1048608 | tf_op jit(solution)/shard_map/all_to_all | solution.py:103
  59.9 0.5 convolution_bitcast_fusion
  60.4 0.7 slice_subtract_fusion
  61.1 0.6 dynamic_slice.3
  62.4 88.2 %all-reduce.4.cloned.1.call-done = (f32[1,128,128]{1,2,0:T(8,128)}, f32[1,128,128]{1,2,0:T(8,128)}) async-done(((f32[1,128,128]{1,2,0:T(8,128)}, f32[1,128,128]{1,2,0:T(8,128)}), (f32[1,128,128]{1,2,0:T(8,128)}, f32[1,128,128]{1,2,0:T(8,128)})) %all-reduce.4.cloned.1.call-update) | async-done | bytes 131088 | tf_op jit(solution)/shard_map/psum | solution.py:112
  150.6 0.8 neg.17
  151.4 0.9 fusion.24
  152.5 1.0 fusion.25
  153.5 11.7 %custom-call.20 = f32[1,128,128]{2,1,0:T(8,128)S(1)} custom-call(f32[1,128,128]{2,1,0:T(8,128)S(1)} %cholesky.114), custom_call_target="Cholesky" | custom-call | tf_op jit(solution)/shard_map/jit(cholesky)/cholesky | solution.py:114
  165.3 9.8 %custom-call.21 = f32[1,1,128,128]{2,3,1,0:T(8,128)S(1)} custom-call(f32[1,1,128,128]{3,2,1,0:T(8,128)S(1)} %get-tuple-element.46), custom_call_target="InvertDiagBlocksLowerTriangular" | custom-call | tf_op jit(solution)/shard_map/jit(cholesky)/cholesky | solution.py:114
  175.3 0.3 fusion.15
  175.6 11.7 %custom-call.22 = f32[1,128,128]{2,1,0:T(8,128)S(1)} custom-call(f32[1,128,128]{2,1,0:T(8,128)S(1)} %fusion.15), custom_call_target="Cholesky" | custom-call | tf_op jit(solution)/shard_map/jit(cholesky)/cholesky | solution.py:114
  187.6 0.7 compare_reduce_fusion
  189.7 4.3 %while.1 = (s32[]{:T(128)}, f32[1,256,256]{1,2,0:T(8,128)S(1)}, s32[2,2]{1,0:T(2,128)S(1)}, f32[2,1,128,128]{3,2,1,0:T(8,128)S(1)}, s32[]{:T(128)}) while((s32[]{:T(128)}, f32[1,256,256]{1,2,0:T(8,128)S(1)}, s32[2,2]{1,0:T(2,128)S(1)}, f32[2,1,128,128]{3,2,1,0:T(8,128)S(1)}, s32[]{:T(128)}) %tuple.37), condition=%wide.while_cond, body=%wide.while_body.sunk | while | flops 2 | bytes 393325 | solution.py:79
  189.9 0.6 fusion.71
  190.5 1.3 constant_dynamic-slice_fusion.5
  192.0 0.6 fusion.71
  192.6 1.3 constant_dynamic-slice_fusion.5
  194.0 19.7 %custom-call.23 = f32[1,2,128,128]{2,3,1,0:T(8,128)S(1)} custom-call(f32[1,2,128,128]{3,2,1,0:T(8,128)S(1)} %bitcast.108), custom_call_target="InvertDiagBlocksLowerTriangular" | custom-call | tf_op jit(solution)/shard_map/vmap(jit(_solve_triangular))/triangular_solve | solution.py:79
  213.7 0.5 fusion.31
  214.2 0.4 convolution_subtract_fusion.1
  214.7 0.3 fusion.40
  215.7 1.4 convolution_convert_fusion.1
  (40 shorter events, 1.9 us)
Async XLA Ops:
  7.5 5.8 %collective-permute-start = (bf16[8,32,7]{2,1,0:T(8,128)(2,1)S(1)}, bf16[8,32,7]{2,1,0:T(8,128)(2,1)S(1)}, u32[]{:S(2)}, u32[]{:S(2)}) collective-permute-start(bf16[8,32,7]{2,1,0:T(8,128)(2,1)S(1)} %slice.142), channel_id=1, source_target_pairs={{0,1},{1,2},{2,3},{3,4},{4,5},{5,6},{6,7},{7,8},{8,9},{9,10},{10,1... | collective-permute-start | bytes 10760 | tf_op jit(solution)/shard_map/ppermute | solution.py:21
  20.7 11.3 %copy-start = (f32[2,128]{1,0:T(2,128)S(1)}, f32[2,128]{1,0:T(2,128)}, u32[]{:S(2)}) copy-start(f32[2,128]{1,0:T(2,128)} %param.7) | copy-start | bytes 3076
  22.3 37.5 %all-to-all-start = ((bf16[16,2,8,2048]{3,2,1,0:T(8,128)(2,1)}), bf16[16,2,8,2048]{3,2,1,0:T(8,128)(2,1)S(1)}, u32[]{:S(2)}, u32[]{:S(2)}) async-start(bf16[16,2,8,2048]{3,2,1,0:T(8,128)(2,1)} %copy.27), calls=%async_computation | async-start | bytes 2097152 | tf_op jit(solution)/shard_map/all_to_all | solution.py:103
  31.8 118.8 %all-reduce.4.cloned.1.call-start = ((), (), s32[]{:S(2)}) async-start(), calls=%async_computation.1 | async-start | bytes 262144 | tf_op jit(solution)/shard_map/psum | solution.py:112
  32.0 29.0 %copy-start.2 = (s32[128]{0:T(128)S(1)}, s32[128]{0:T(128)}, u32[]{:S(2)}) copy-start(s32[128]{0:T(128)} %param.8) | copy-start | bytes 1540
  32.1 29.1 %copy-start.1 = (s32[16]{0:T(128)S(1)}, s32[16]{0:T(128)}, u32[]{:S(2)}) copy-start(s32[16]{0:T(128)} %param.9) | copy-start | bytes 196
Sparse Core Ops, SparseCore 0:
  61.2 89.3 all-reduce.3
where the time goes:
time: 225 us; the launch traced here: 224 us
  waiting for transfers between devices  116 us (52%)
  other arithmetic  59.6 us (26%)
  between operations  15.6 us (7%)
  starting transfers between devices  13.8 us (6%)
  matrix products  10 us (4%)
  local copies, waits for them, and re-layouts  8.83 us (4%)
    psum x1, waiting for transfers between devices, on_device(): sym_part, skew_part = lax.psum((sym_part, skew_part), 'seg')  88.2 us
    another operation x6, other arithmetic, on_device(): factor = jnp.linalg.cholesky(covariance)  34 us
    all_to_all x1, waiting for transfers between devices, on_device(): lax.all_to_all(spectra, 'stn', split_axis=0, concat_axis=2, tiled=True)  27.7 us
    another operation x3, other arithmetic, solve_weights(): jax.scipy.linalg.solve_triangular(factor, whitened, lower=True, trans=1)  19.7 us
    all_to_all x1, starting transfers between devices, on_device(): lax.all_to_all(spectra, 'stn', split_axis=0, concat_axis=2, tiled=True)  9.53 us
    dot_general x1, matrix products, channelize(): jnp.einsum('jap,spt->jast', dft_table, filtered, precision=lax.Precision....  5.83 us
  transfers between devices with their start and end apart: 3, of which 2 were waited for; matrix products, arithmetic and copies ran while one was open for 1% of the time, Pallas kernels for 0%

commit v1 on v0

v1 whole, which is shorter than its diff:
```python
import functools
import math

import jax
import jax.numpy as jnp
from jax import lax
from jax.experimental import pallas as pl
from jax.experimental.pallas import tpu as pltpu
from jax.sharding import PartitionSpec as P

C = 16
TAPS = 8
B = 128
DIRS = 360
S = 128
SEG = 16


loading_level = 0.1
full_turn = 2.0 * math.pi
HIGHEST = lax.Precision.HIGHEST
MESH = pl.DeviceIdType.MESH


def passed_along(value, axis, by):
    length = lax.axis_size(axis)
    pairs = [(i, i + by) for i in range(length) if 0 <= i + by < length]
    return lax.ppermute(value, axis, pairs)


def dft_tables(chan_table):
    frame_width = 2 * C
    phase_index = jnp.remainder(
        chan_table[:, None] * jnp.arange(frame_width, dtype=jnp.int32)[None, :], frame_width
    )
    angles = phase_index.astype(jnp.float32) * (full_turn / frame_width)
    return jnp.stack([jnp.cos(angles), -jnp.sin(angles)], axis=1)


def filter_block(station_block, filter_taps):
    snap_count = station_block.shape[2] - (TAPS - 1)
    widened = station_block.astype(jnp.float32)
    summed = jnp.zeros((station_block.shape[0], station_block.shape[1], snap_count), jnp.float32)
    for tap_index in range(TAPS):
        offset = TAPS - 1 - tap_index
        summed = (
            summed
            + filter_taps[tap_index][None, :, None] * widened[:, :, offset : offset + snap_count]
        )
    return summed


def channelize(filtered, dft_table):
    return jnp.einsum("jap,spt->jast", dft_table, filtered, precision=HIGHEST).astype(
        jnp.bfloat16
    )


def steering(positions, beam_dirs, channel):
    bearing = beam_dirs.astype(jnp.float32) * (full_turn / DIRS)
    frequency = 1.0 + channel.astype(jnp.float32) / C
    path_delay = (
        positions[0][:, None] * jnp.cos(bearing)[None, :]
        + positions[1][:, None] * jnp.sin(bearing)[None, :]
    )
    phases = full_turn * frequency * path_delay
    return jnp.concatenate([jnp.cos(phases), jnp.sin(phases)], axis=0)


def seg_sum_kernel(part_ref, sum_ref, landed, send_a, recv_a, send_b, recv_b):
    me = lax.axis_index("seg")
    barrier = pltpu.get_barrier_semaphore()
    peers = [lax.rem(me + d, SEG) for d in range(1, SEG)]
    for peer in peers:
        pl.semaphore_signal(barrier, inc=1, device_id={"seg": peer}, device_id_type=MESH)
    pl.semaphore_wait(barrier, SEG - 1)
    spread = []
    for d, peer in enumerate(peers):
        copy = pltpu.make_async_remote_copy(
            src_ref=part_ref.at[peer],
            dst_ref=landed.at[d],
            send_sem=send_a.at[d],
            recv_sem=recv_a.at[d],
            device_id={"seg": peer},
            device_id_type=MESH,
        )
        copy.start()
        spread.append(copy)
    total = part_ref[me]
    for d, copy in enumerate(spread):
        copy.wait_recv()
        total = total + landed[d]
    sum_ref[me] = total
    shared = []
    for d, peer in enumerate(peers):
        copy = pltpu.make_async_remote_copy(
            src_ref=sum_ref.at[me],
            dst_ref=sum_ref.at[me],
            send_sem=send_b.at[d],
            recv_sem=recv_b.at[d],
            device_id={"seg": peer},
            device_id_type=MESH,
        )
        copy.start()
        shared.append(copy)
    for copy in spread:
        copy.wait_send()
    for copy in shared:
        copy.wait()


def seg_sum(part):
    rows = S // SEG
    vmem = pl.BlockSpec(memory_space=pltpu.VMEM)
    return pl.pallas_call(
        seg_sum_kernel,
        out_shape=jax.ShapeDtypeStruct((SEG, rows, S), jnp.float32),
        in_specs=[vmem],
        out_specs=vmem,
        scratch_shapes=[
            pltpu.VMEM((SEG - 1, rows, S), jnp.float32),
            pltpu.SemaphoreType.DMA((SEG - 1,)),
            pltpu.SemaphoreType.DMA((SEG - 1,)),
            pltpu.SemaphoreType.DMA((SEG - 1,)),
            pltpu.SemaphoreType.DMA((SEG - 1,)),
        ],
        compiler_params=pltpu.CompilerParams(collective_id=1, has_side_effects=True),
        name="seg_sum",
    )(part.reshape(SEG, rows, S)).reshape(S, S)


def invert_hermitian(hr_ref, hi_ref):
    groups = S // 8
    lane = lax.broadcasted_iota(jnp.int32, (8, S), 1)
    row = lax.broadcasted_iota(jnp.int32, (8, S), 0)

    def trip(_, carry):
        hr = [hr_ref[pl.ds(8 * g, 8), :] for g in range(groups)]
        hi = [hi_ref[pl.ds(8 * g, 8), :] for g in range(groups)]
        pr, pi = hr[0], hi[0]
        for i in range(8):
            cr, ci = pr[:, i : i + 1], pi[:, i : i + 1]
            inv = 1.0 / pr[i : i + 1, i : i + 1]
            at = lane[0:1] == i
            rr = jnp.where(at, inv, pr[i : i + 1, :] * inv)
            ri = jnp.where(at, 0.0, pi[i : i + 1, :] * inv)
            br = jnp.where(lane == i, 0.0, pr)
            bi = jnp.where(lane == i, 0.0, pi)
            nr = br - (cr * rr - ci * ri)
            ni = bi - (cr * ri + ci * rr)
            pr = jnp.where(row == i, rr, nr)
            pi = jnp.where(row == i, ri, ni)
        for g in range(1, groups):
            ar = jnp.where(lane < 8, 0.0, hr[g])
            ai = jnp.where(lane < 8, 0.0, hi[g])
            for i in range(8):
                cr, ci = hr[g][:, i : i + 1], hi[g][:, i : i + 1]
                rr, ri = pr[i : i + 1, :], pi[i : i + 1, :]
                ar = ar - (cr * rr - ci * ri)
                ai = ai - (cr * ri + ci * rr)
            hr_ref[pl.ds(8 * (g - 1), 8), :] = pltpu.roll(ar, S - 8, 1)
            hi_ref[pl.ds(8 * (g - 1), 8), :] = pltpu.roll(ai, S - 8, 1)
        hr_ref[pl.ds(S - 8, 8), :] = pltpu.roll(pr, S - 8, 1)
        hi_ref[pl.ds(S - 8, 8), :] = pltpu.roll(pi, S - 8, 1)
        return carry

    lax.fori_loop(0, groups, trip, 0)


def beam_kernel(snap_total, packed_ref, steer_ref, stacked_ref, out_ref, hr_ref, hi_ref):
    packed = packed_ref[...]
    turned = packed.T
    row = lax.broadcasted_iota(jnp.int32, (S, S), 0)
    lane = lax.broadcasted_iota(jnp.int32, (S, S), 1)
    upper = lane > row
    diag = lane == row
    sym = jnp.where(upper, turned, packed) / snap_total
    skew = jnp.where(upper, packed, -turned) / snap_total
    hr_ref[...] = sym + jnp.where(diag, loading_level, 0.0)
    hi_ref[...] = jnp.where(diag, 0.0, skew)
    invert_hermitian(hr_ref, hi_ref)
    vr, vi = steer_ref[0:S], steer_ref[S : 2 * S]
    both = jnp.concatenate([vr, vi], axis=1)
    by_real = jnp.dot(hr_ref[...], both, precision=HIGHEST, preferred_element_type=jnp.float32)
    by_imag = jnp.dot(hi_ref[...], both, precision=HIGHEST, preferred_element_type=jnp.float32)
    wr = by_real[:, :B] - by_imag[:, B:]
    wi = by_real[:, B:] + by_imag[:, :B]
    power = jnp.sum(vr * wr + vi * wi, axis=0, keepdims=True)
    scale = 1.0 / jnp.sqrt(power)
    wr = (wr * scale).astype(jnp.bfloat16)
    wi = (wi * scale).astype(jnp.bfloat16)
    weights = jnp.concatenate([wr, wi], axis=0)
    swapped = jnp.concatenate([-wi, wr], axis=0)
    mix = jnp.concatenate([weights, swapped], axis=1).T
    width = 512

    def tile(n, carry):
        at = pl.ds(pl.multiple_of(n * width, width), width)
        res = jnp.dot(mix, stacked_ref[:, at], preferred_element_type=jnp.float32)
        out_ref[:, at] = res.astype(jnp.bfloat16)
        return carry

    lax.fori_loop(0, stacked_ref.shape[1] // width, tile, 0)


def beams(packed, steer, stacked, snap_total):
    vmem = pl.BlockSpec(memory_space=pltpu.VMEM)
    return pl.pallas_call(
        functools.partial(beam_kernel, snap_total),
        out_shape=jax.ShapeDtypeStruct((2 * B, stacked.shape[1]), jnp.bfloat16),
        in_specs=[vmem, vmem, vmem],
        out_specs=vmem,
        scratch_shapes=[pltpu.VMEM((S, S), jnp.float32), pltpu.VMEM((S, S), jnp.float32)],
        name="beams",
    )(packed, steer, stacked)


def on_device(voltages, filter_taps, positions, beam_dirs, chan_table):
    last_frames = voltages[:, :, voltages.shape[2] - (TAPS - 1) :]
    earlier = passed_along(last_frames, "seg", 1)
    extended = jnp.concatenate([earlier, voltages], axis=2)
    filtered = filter_block(extended, filter_taps)
    spectra = channelize(filtered, dft_tables(chan_table))
    turned = lax.all_to_all(spectra, "stn", split_axis=0, concat_axis=2, tiled=True)
    snap_count = turned.shape[3]
    stacked = turned.reshape(2 * S, snap_count)
    gram = jnp.einsum("at,bt->ab", stacked, stacked, preferred_element_type=jnp.float32)
    sym_part = gram[:S, :S] + gram[S:, S:]
    skew_part = gram[S:, :S] - gram[:S, S:]
    upper = jnp.arange(S)[None, :] > jnp.arange(S)[:, None]
    packed = seg_sum(jnp.where(upper, skew_part, sym_part))
    channel = lax.dynamic_index_in_dim(chan_table, lax.axis_index("stn"), keepdims=False)
    steer = steering(positions, beam_dirs, channel)
    beam_out = beams(packed, steer, stacked, float(snap_count * SEG))
    return beam_out.reshape(1, 2, B, snap_count)


def solution(mesh):
    return jax.shard_map(
        on_device,
        mesh=mesh,
        in_specs=(P("stn", None, "seg"), P(), P(), P(), P()),
        out_specs=P("stn", None, None, "seg"),
        check_vma=False,
    )
```

time: 225 us -> 90.1 us (0.40)
  waiting for transfers between devices: 116 us -> 25.7 us
  other arithmetic: 59.6 us -> 4.04 us
  Pallas kernels: 0 us -> 35.2 us
  between operations: 15.6 us -> 0.77 us
  local copies, waits for them, and re-layouts: 8.83 us -> 4.23 us
  matrix products: 10 us -> 6.29 us
    psum x1 -> x0, waiting for transfers between devices: 88.2 us -> none  [on_device(): sym_part, skew_part = lax.psum((sym_part, skew_part), 'seg')]
    another operation x9 -> x0, other arithmetic: 53.7 us -> none  [the longest x6 34 us: on_device(): factor = jnp.linalg.cholesky(covariance)]
    pallas_call x0 -> x2, Pallas kernels: none -> 35.2 us  [the longest x1 18.6 us: beams(): pl.pallas_call(functools.partial(beam_kernel, snap_total), out_shape=jax....]
    another operation x18 -> x0, local copies, waits for them, and re-layouts: 4.46 us -> none
    another operation x8 -> x0, matrix products: 2.31 us -> none  [the longest x3 1.22 us: solve_weights(): whitened = jax.scipy.linalg.solve_triangular(factor, steer, lower=True)]
    dot_general x3 -> x2, matrix products: 7.73 us -> 6.29 us  [the longest x1 5.82 us: channelize(): jnp.einsum('jap,spt->jast', dft_table, filtered, precision=HIGHEST)]
  transfers between devices with their start and end apart: 3 -> 2, of which waited for: 2 -> 1; matrix products, arithmetic and copies ran while one was open for 1% -> 4% of each run, Pallas kernels for 0% -> 0%
where the time goes in v1:
time: 90.1 us; the launch traced here: 89.8 us
  Pallas kernels  35.2 us (39%)
  waiting for transfers between devices  25.7 us (29%)
  starting transfers between devices  13.5 us (15%)
  matrix products  6.29 us (7%)
  local copies, waits for them, and re-layouts  4.23 us (5%)
  other arithmetic  4.04 us (4%)
    all_to_all x1, waiting for transfers between devices, on_device(): lax.all_to_all(spectra, 'stn', split_axis=0, concat_axis=2, tiled=True)  25.6 us
    pallas_call x1, Pallas kernels, beams(): pl.pallas_call(functools.partial(beam_kernel, snap_total), out_shape=jax....  18.6 us
    pallas_call x1, Pallas kernels, seg_sum(): pl.pallas_call(seg_sum_kernel, out_shape=jax.ShapeDtypeStruct((SEG, rows,...  16.6 us
    all_to_all x1, starting transfers between devices, on_device(): lax.all_to_all(spectra, 'stn', split_axis=0, concat_axis=2, tiled=True)  9.52 us
    dot_general x1, matrix products, channelize(): jnp.einsum('jap,spt->jast', dft_table, filtered, precision=HIGHEST)  5.82 us
    ppermute x1, starting transfers between devices, passed_along(): return lax.ppermute(value, axis, pairs)  4.02 us
  transfers between devices with their start and end apart: 2, of which 1 were waited for; matrix products, arithmetic and copies ran while one was open for 4% of the time, Pallas kernels for 0%

profile of v1, /device:TPU:1, one launch (start us, length us, event | category | flops | bytes accessed | tf_op | source)
XLA Modules:
  0.0 89.8 jit_solution(7154792519703579844)
XLA Ops:
  0.0 0.9 %slice.70 = bf16[8,32,7]{2,1,0:T(8,128)(2,1)S(1)} slice(bf16[8,32,2048]{2,1,0:T(8,128)(2,1)} %param.5), slice={[0:8], [0:32], [2041:2048]} | slice | bytes 7168 | tf_op jit(solution)/shard_map/slice | solution.py:219
  0.9 4.0 %collective-permute-start = (bf16[8,32,7]{2,1,0:T(8,128)(2,1)S(1)}, bf16[8,32,7]{2,1,0:T(8,128)(2,1)S(1)}, u32[]{:S(2)}, u32[]{:S(2)}) collective-permute-start(bf16[8,32,7]{2,1,0:T(8,128)(2,1)S(1)} %slice.70), channel_id=1, source_target_pairs={{0,1},{1,2},{2,3},{3,4},{4,5},{5,6},{6,7},{7,8},{8,9},{9,10},{10,1... | collective-permute-start | bytes 10760 | tf_op jit(solution)/shard_map/ppermute | solution.py:28
  5.0 0.8 fusion.35
  5.7 1.0 %slice_bitcast_fusion.9 = (f32[32]{0:T(128)S(1)}, f32[32]{0:T(128)S(1)}, f32[32]{0:T(128)S(1)}, f32[32]{0:T(128)S(1)}, f32[32]{0:T(128)S(1)}, /*index=5*/f32[32]{0:T(128)S(1)}, f32[32]{0:T(128)S(1)}, f32[32]{0:T(128)S(1)}) fusion(f32[8,32]{1,0:T(8,128)} %param.6), kind=kLoop, calls=%fused_computation.59 | loop fusion | bytes 2048 | tf_op jit(solution)/shard_map/mul | solution.py:48
  6.7 0.0 collective-permute-done
  6.7 1.6 %maximum_convert_fusion = f32[8,32,2055]{2,1,0:T(8,128)S(1)} fusion(bf16[8,32,2048]{2,1,0:T(8,128)(2,1)} %param.5, bf16[8,32,7]{2,1,0:T(8,128)(2,1)S(1)} %collective-permute-done), kind=kLoop, calls=%fused_computation.17 | loop fusion | flops 2104320 | bytes 3156480 | tf_op jit(solution)/shard_map/convert_element_type | solution.py:42
  8.3 5.8 %convolution_convert_fusion = bf16[16,2,8,2048]{3,0,2,1:T(8,128)(2,1)S(1)} fusion(f32[8,32,2055]{2,1,0:T(8,128)S(1)} %maximum_convert_fusion, f32[32]{0:T(128)S(1)} %get-tuple-element.11, f32[32]{0:T(128)S(1)} %get-tuple-element.12, f32[32]{0:T(128)S(1)} %get-tuple-element.6, f32[32]{0:T(128)S(1)} %get-tuple-element.7, f32[32]{0:T(128)S(1)} %get-tuple-element.8, ...), kind=kOutput, calls=%fused_computation | convolution fusion | flops 209716224 | bytes 17846272 | tf_op jit(solution)/shard_map/jap,spt->jast/dot_general | solution.py:54
  14.2 0.0 copy-start.2
  14.2 0.0 copy-start.3
  14.2 0.0 copy-start.1
  14.2 1.5 %copy.7 = bf16[16,2,8,2048]{3,2,1,0:T(8,128)(2,1)} copy(bf16[16,2,8,2048]{3,0,2,1:T(8,128)(2,1)S(1)} %convolution_convert_fusion) | data formatting | bytes 2097152 | tf_op jit(solution)/shard_map/convert_element_type | solution.py:54
  15.8 9.5 %all-to-all-start = ((bf16[16,2,8,2048]{3,2,1,0:T(8,128)(2,1)}), bf16[16,2,8,2048]{3,2,1,0:T(8,128)(2,1)S(1)}, u32[]{:S(2)}, u32[]{:S(2)}) async-start(bf16[16,2,8,2048]{3,2,1,0:T(8,128)(2,1)} %copy.7), calls=%async_computation | async-start | bytes 2097152 | tf_op jit(solution)/shard_map/all_to_all | solution.py:224
  25.3 0.0 copy-done.2
  25.3 0.7 dynamic_slice.4
  26.6 0.0 copy-done.3
  26.6 0.0 copy-done.1
  26.6 0.3 fusion.26
  27.0 0.6 pad_maximum_fusion.steer_ref
  27.6 25.6 %all-to-all-done = bf16[16,2,8,2048]{3,2,1,0:T(8,128)(2,1)S(1)} async-done(((bf16[16,2,8,2048]{3,2,1,0:T(8,128)(2,1)}), bf16[16,2,8,2048]{3,2,1,0:T(8,128)(2,1)S(1)}, u32[]{:S(2)}, u32[]{:S(2)}) %all-to-all-start) | async-done | bytes 1048608 | tf_op jit(solution)/shard_map/all_to_all | solution.py:224
  53.3 0.1 copy.8
  53.4 0.0 copy-start
  53.4 0.5 fusion.39
  53.9 0.6 fusion.24.part_ref
  54.5 16.6 %seg_sum.1 = f32[16,8,128]{2,1,0:T(8,128)} custom-call(f32[16,8,128]{2,1,0:T(8,128)} %fusion.24.part_ref), custom_call_target="tpu_custom_call" | custom-call | tf_op jit(solution)/shard_map/seg_sum/pallas_call | solution.py:115
  71.2 0.0 copy-done
  71.2 18.6 %beams.1 = bf16[256,2048]{1,0:T(8,128)(2,1)} custom-call(f32[128,128]{1,0:T(8,128)} %bitcast.42, f32[256,128]{1,0:T(8,128)} %pad_maximum_fusion.steer_ref, bf16[256,2048]{1,0:T(8,128)(2,1)} %bitcast.40), custom_call_target="tpu_custom_call" | custom-call | tf_op jit(solution)/shard_map/beams/pallas_call | solution.py:208
  (2 shorter events, 0.0 us)
Async XLA Ops:
  0.9 5.8 %collective-permute-start = (bf16[8,32,7]{2,1,0:T(8,128)(2,1)S(1)}, bf16[8,32,7]{2,1,0:T(8,128)(2,1)S(1)}, u32[]{:S(2)}, u32[]{:S(2)}) collective-permute-start(bf16[8,32,7]{2,1,0:T(8,128)(2,1)S(1)} %slice.70), channel_id=1, source_target_pairs={{0,1},{1,2},{2,3},{3,4},{4,5},{5,6},{6,7},{7,8},{8,9},{9,10},{10,1... | collective-permute-start | bytes 10760 | tf_op jit(solution)/shard_map/ppermute | solution.py:28
  14.2 11.1 %copy-start.2 = (s32[16]{0:T(128)S(1)}, s32[16]{0:T(128)}, u32[]{:S(2)}) copy-start(s32[16]{0:T(128)} %param.9) | copy-start | bytes 196
  14.2 12.4 %copy-start.3 = (s32[128]{0:T(128)S(1)}, s32[128]{0:T(128)}, u32[]{:S(2)}) copy-start(s32[128]{0:T(128)} %param.8) | copy-start | bytes 1540
  14.2 12.4 %copy-start.1 = (f32[2,128]{1,0:T(2,128)S(1)}, f32[2,128]{1,0:T(2,128)}, u32[]{:S(2)}) copy-start(f32[2,128]{1,0:T(2,128)} %param.7) | copy-start | bytes 3076
  15.8 37.5 %all-to-all-start = ((bf16[16,2,8,2048]{3,2,1,0:T(8,128)(2,1)}), bf16[16,2,8,2048]{3,2,1,0:T(8,128)(2,1)S(1)}, u32[]{:S(2)}, u32[]{:S(2)}) async-start(bf16[16,2,8,2048]{3,2,1,0:T(8,128)(2,1)} %copy.7), calls=%async_computation | async-start | bytes 2097152 | tf_op jit(solution)/shard_map/all_to_all | solution.py:224
  53.4 17.8 %copy-start = (bf16[1,2,16,8,2048]{4,3,2,1,0:T(8,128)(2,1)}, bf16[1,2,16,8,2048]{4,3,2,1,0:T(8,128)(2,1)S(1)}, u32[]{:S(2)}) copy-start(bf16[1,2,16,8,2048]{4,3,2,1,0:T(8,128)(2,1)S(1)} %copy.8) | copy-start | bytes 3145732

commit v2 on v1

v2 whole, which is shorter than its diff:
```python
import functools
import math

import jax
import jax.numpy as jnp
from jax import lax
from jax.experimental import pallas as pl
from jax.experimental.pallas import tpu as pltpu
from jax.sharding import PartitionSpec as P

C = 16
TAPS = 8
B = 128
DIRS = 360
S = 128
SEG = 16
STN = 16
CHUNKS = 4
PAD = 128


loading_level = 0.1
full_turn = 2.0 * math.pi
HIGHEST = lax.Precision.HIGHEST
MESH = pl.DeviceIdType.MESH


def front_kernel(
    v_ref, taps_ref, pos_ref, dirs_ref, chan_ref,
    packed_ref, steer_ref, out_ref,
    vbuf, spread, spec, land, gram, part, landed,
    vsem, osem, hsem, send_x, recv_x, send_a, recv_a, send_b, recv_b,
):
    stn, seg = lax.axis_index("stn"), lax.axis_index("seg")
    stn_peers = [lax.rem(stn + d, STN) for d in range(1, STN)]
    seg_peers = [lax.rem(seg + d, SEG) for d in range(1, SEG)]
    local = v_ref.shape[0]
    snaps = v_ref.shape[2]
    wide = snaps // CHUNKS
    frame = 2 * C

    barrier = pltpu.get_barrier_semaphore()
    for peer in stn_peers:
        pl.semaphore_signal(barrier, inc=1, device_id={"stn": peer}, device_id_type=MESH)
    for peer in seg_peers:
        pl.semaphore_signal(barrier, inc=1, device_id={"seg": peer}, device_id_type=MESH)
    fetches = []
    for c in range(CHUNKS):
        fetch = pltpu.make_async_copy(
            v_ref.at[:, :, pl.ds(c * wide, wide)],
            vbuf.at[:, :, pl.ds(PAD + c * wide, wide)],
            vsem.at[c],
        )
        fetch.start()
        fetches.append(fetch)

    row = lax.broadcasted_iota(jnp.int32, (frame, TAPS * frame), 0)
    lane = lax.broadcasted_iota(jnp.int32, (frame, TAPS * frame), 1)
    channel_of = jnp.zeros((frame, TAPS * frame), jnp.int32)
    for j in range(C):
        channel_of = jnp.where(row // 2 == j, chan_ref[j], channel_of)
    phase_index = jnp.bitwise_and(channel_of * jnp.bitwise_and(lane, frame - 1), frame - 1)
    angles = phase_index.astype(jnp.float32) * (full_turn / frame)
    table = jnp.where(row % 2 == 0, jnp.cos(angles), -jnp.sin(angles))
    taps = jnp.concatenate([taps_ref[m : m + 1, :] for m in range(TAPS)], axis=1)
    mixed = table * taps
    high = mixed.astype(jnp.bfloat16)
    low = (mixed - high.astype(jnp.float32)).astype(jnp.bfloat16)
    mixed = jnp.concatenate([high, low], axis=0)

    def channelize_chunk(c):
        def station(s, carry):
            x = vbuf[s, :, pl.ds(c * wide, wide + PAD)]
            moved = [x[:, PAD - m : PAD - m + wide] for m in range(TAPS)]
            res = jnp.dot(
                mixed, jnp.concatenate(moved, axis=0), preferred_element_type=jnp.float32
            )
            res = res[:frame] + res[frame:]
            for q in range(wide // PAD):
                spread[q, pl.ds(pl.multiple_of(s * frame, frame), frame), :] = res[
                    :, q * PAD : (q + 1) * PAD
                ]
            return carry

        lax.fori_loop(0, local, station, 0, unroll=2)
        for j in range(C):
            for a in range(2):
                for q in range(wide // PAD):
                    picked = spread[q, pl.ds(2 * j + a, local, stride=frame), :]
                    spec[c, j, a, :, q * PAD : (q + 1) * PAD] = picked.astype(jnp.bfloat16)

    def send_chunk(c):
        copies = []
        for d, peer in enumerate(stn_peers):
            copy = pltpu.make_async_remote_copy(
                src_ref=spec.at[c, peer],
                dst_ref=land.at[:, stn, :, pl.ds(c * wide, wide)],
                send_sem=send_x.at[c, d],
                recv_sem=recv_x.at[c, d],
                device_id={"stn": peer},
                device_id_type=MESH,
            )
            copy.start()
            copies.append(copy)
        land[:, stn, :, pl.ds(c * wide, wide)] = spec[c, stn]
        return copies

    order = list(range(1, CHUNKS)) + [0]
    for c in range(2):
        fetches[c].wait()
    channelize_chunk(order[0])
    pl.semaphore_wait(barrier, STN - 1 + SEG - 1)
    halo = pltpu.make_async_remote_copy(
        src_ref=v_ref.at[:, :, pl.ds(snaps - PAD, PAD)],
        dst_ref=vbuf.at[:, :, pl.ds(0, PAD)],
        send_sem=hsem.at[0],
        recv_sem=hsem.at[1],
        device_id={"seg": seg_peers[0]},
        device_id_type=MESH,
    )
    halo.start()
    sent = {order[0]: send_chunk(order[0])}
    for c in order[1:]:
        if c >= 2:
            fetches[c].wait()
        if c == 0:
            halo.wait()

            @pl.when(seg == 0)
            def _():
                vbuf[:, :, 0:PAD] = jnp.zeros((local, frame, PAD), jnp.bfloat16)

        channelize_chunk(c)
        sent[c] = send_chunk(c)

    bearing = dirs_ref[...].astype(jnp.float32) * (full_turn / DIRS)
    frequency = 1.0 + chan_ref[stn].astype(jnp.float32) / C
    east = jnp.broadcast_to(pos_ref[0:1, :], (S, S)).T
    north = jnp.broadcast_to(pos_ref[1:2, :], (S, S)).T
    phases = (full_turn * frequency) * (east * jnp.cos(bearing) + north * jnp.sin(bearing))
    steer_ref[0:S, :] = jnp.cos(phases)
    steer_ref[S : 2 * S, :] = jnp.sin(phases)

    stores = []
    for n, c in enumerate(order):
        for copy in sent[c]:
            copy.wait_recv()
        at = pl.ds(c * wide, wide)
        store = pltpu.make_async_copy(land.at[:, :, :, at], out_ref.at[:, :, :, at], osem.at[c])
        store.start()
        stores.append(store)
        block = land[:, :, :, at].reshape(2 * S, wide)
        term = lax.dot_general(
            block, block, (((1,), (1,)), ((), ())), preferred_element_type=jnp.float32
        )
        if n == 0:
            gram[...] = term
        else:
            gram[...] += term

    sym = gram[0:S, 0:S] + gram[S : 2 * S, S : 2 * S]
    skew = gram[S : 2 * S, 0:S] - gram[0:S, S : 2 * S]
    row = lax.broadcasted_iota(jnp.int32, (S, S), 0)
    lane = lax.broadcasted_iota(jnp.int32, (S, S), 1)
    part[...] = jnp.where(lane > row, skew, sym).reshape(part.shape)

    spread_out = []
    for d, peer in enumerate(seg_peers):
        copy = pltpu.make_async_remote_copy(
            src_ref=part.at[peer],
            dst_ref=landed.at[d],
            send_sem=send_a.at[d],
            recv_sem=recv_a.at[d],
            device_id={"seg": peer},
            device_id_type=MESH,
        )
        copy.start()
        spread_out.append(copy)
    total = part[seg]
    for d, copy in enumerate(spread_out):
        copy.wait_recv()
        total = total + landed[d]
    packed_ref[seg] = total
    shared = []
    for d, peer in enumerate(seg_peers):
        copy = pltpu.make_async_remote_copy(
            src_ref=packed_ref.at[seg],
            dst_ref=packed_ref.at[seg],
            send_sem=send_b.at[d],
            recv_sem=recv_b.at[d],
            device_id={"seg": peer},
            device_id_type=MESH,
        )
        copy.start()
        shared.append(copy)
    for c in order:
        for copy in sent[c]:
            copy.wait_send()
    for store in stores:
        store.wait()
    for copy in spread_out:
        copy.wait_send()
    for copy in shared:
        copy.wait()


def front(voltages, filter_taps, positions, beam_dirs, chan_table):
    local, frame, snaps = voltages.shape
    wide = snaps // CHUNKS
    rows = S // SEG
    vmem = pl.BlockSpec(memory_space=pltpu.VMEM)
    hbm = pl.BlockSpec(memory_space=pl.ANY)
    smem = pl.BlockSpec(memory_space=pltpu.SMEM)
    dma = pltpu.SemaphoreType.DMA
    return pl.pallas_call(
        front_kernel,
        out_shape=(
            jax.ShapeDtypeStruct((SEG, rows, S), jnp.float32),
            jax.ShapeDtypeStruct((2 * S, B), jnp.float32),
            jax.ShapeDtypeStruct((2, STN, local, snaps), jnp.bfloat16),
        ),
        in_specs=[hbm, vmem, vmem, vmem, smem],
        out_specs=(vmem, vmem, hbm),
        scratch_shapes=[
            pltpu.VMEM((local, frame, PAD + snaps), jnp.bfloat16),
            pltpu.VMEM((wide // PAD, local * frame, PAD), jnp.float32),
            pltpu.VMEM((CHUNKS, STN, 2, local, wide), jnp.bfloat16),
            pltpu.VMEM((2, STN, local, snaps), jnp.bfloat16),
            pltpu.VMEM((2 * S, 2 * S), jnp.float32),
            pltpu.VMEM((SEG, rows, S), jnp.float32),
            pltpu.VMEM((SEG - 1, rows, S), jnp.float32),
            dma((CHUNKS,)),
            dma((CHUNKS,)),
            dma((2,)),
            dma((CHUNKS, STN - 1)),
            dma((CHUNKS, STN - 1)),
            dma((SEG - 1,)),
            dma((SEG - 1,)),
            dma((SEG - 1,)),
            dma((SEG - 1,)),
        ],
        compiler_params=pltpu.CompilerParams(
            collective_id=1, has_side_effects=True, vmem_limit_bytes=32 * 1024 * 1024
        ),
        name="front",
    )(voltages, filter_taps, positions, beam_dirs.reshape(1, B), chan_table)


def invert_hermitian(hr_ref, hi_ref):
    groups = S // 8
    lane = lax.broadcasted_iota(jnp.int32, (8, S), 1)
    row = lax.broadcasted_iota(jnp.int32, (8, S), 0)

    def trip(_, carry):
        hr = [hr_ref[pl.ds(8 * g, 8), :] for g in range(groups)]
        hi = [hi_ref[pl.ds(8 * g, 8), :] for g in range(groups)]
        pr, pi = hr[0], hi[0]
        for i in range(8):
            cr, ci = pr[:, i : i + 1], pi[:, i : i + 1]
            inv = 1.0 / pr[i : i + 1, i : i + 1]
            at = lane[0:1] == i
            rr = jnp.where(at, inv, pr[i : i + 1, :] * inv)
            ri = jnp.where(at, 0.0, pi[i : i + 1, :] * inv)
            br = jnp.where(lane == i, 0.0, pr)
            bi = jnp.where(lane == i, 0.0, pi)
            nr = br - (cr * rr - ci * ri)
            ni = bi - (cr * ri + ci * rr)
            pr = jnp.where(row == i, rr, nr)
            pi = jnp.where(row == i, ri, ni)
        for g in range(1, groups):
            ar = jnp.where(lane < 8, 0.0, hr[g])
            ai = jnp.where(lane < 8, 0.0, hi[g])
            for i in range(8):
                cr, ci = hr[g][:, i : i + 1], hi[g][:, i : i + 1]
                rr, ri = pr[i : i + 1, :], pi[i : i + 1, :]
                ar = ar - (cr * rr - ci * ri)
                ai = ai - (cr * ri + ci * rr)
            hr_ref[pl.ds(8 * (g - 1), 8), :] = pltpu.roll(ar, S - 8, 1)
            hi_ref[pl.ds(8 * (g - 1), 8), :] = pltpu.roll(ai, S - 8, 1)
        hr_ref[pl.ds(S - 8, 8), :] = pltpu.roll(pr, S - 8, 1)
        hi_ref[pl.ds(S - 8, 8), :] = pltpu.roll(pi, S - 8, 1)
        return carry

    lax.fori_loop(0, groups, trip, 0)


def beam_kernel(snap_total, packed_ref, steer_ref, held_ref, out_ref, hr_ref, hi_ref, stacked_ref, sem):
    fetch = pltpu.make_async_copy(held_ref, stacked_ref, sem)
    fetch.start()
    packed = packed_ref[...]
    turned = packed.T
    row = lax.broadcasted_iota(jnp.int32, (S, S), 0)
    lane = lax.broadcasted_iota(jnp.int32, (S, S), 1)
    upper = lane > row
    diag = lane == row
    sym = jnp.where(upper, turned, packed) / snap_total
    skew = jnp.where(upper, packed, -turned) / snap_total
    hr_ref[...] = sym + jnp.where(diag, loading_level, 0.0)
    hi_ref[...] = jnp.where(diag, 0.0, skew)
    invert_hermitian(hr_ref, hi_ref)
    vr, vi = steer_ref[0:S], steer_ref[S : 2 * S]
    both = jnp.concatenate([vr, vi], axis=1)
    by_real = jnp.dot(hr_ref[...], both, precision=HIGHEST, preferred_element_type=jnp.float32)
    by_imag = jnp.dot(hi_ref[...], both, precision=HIGHEST, preferred_element_type=jnp.float32)
    wr = by_real[:, :B] - by_imag[:, B:]
    wi = by_real[:, B:] + by_imag[:, :B]
    power = jnp.sum(vr * wr + vi * wi, axis=0, keepdims=True)
    scale = 1.0 / jnp.sqrt(power)
    wr = (wr * scale).astype(jnp.bfloat16)
    wi = (wi * scale).astype(jnp.bfloat16)
    weights = jnp.concatenate([wr, wi], axis=0)
    swapped = jnp.concatenate([-wi, wr], axis=0)
    mix = jnp.concatenate([weights, swapped], axis=1).T
    width = 512
    fetch.wait()

    def tile(n, carry):
        at = pl.ds(pl.multiple_of(n * width, width), width)
        res = jnp.dot(mix, stacked_ref[:, at], preferred_element_type=jnp.float32)
        out_ref[:, at] = res.astype(jnp.bfloat16)
        return carry

    lax.fori_loop(0, stacked_ref.shape[1] // width, tile, 0)


def beams(packed, steer, stacked, snap_total):
    vmem = pl.BlockSpec(memory_space=pltpu.VMEM)
    return pl.pallas_call(
        functools.partial(beam_kernel, snap_total),
        out_shape=jax.ShapeDtypeStruct((2 * B, stacked.shape[1]), jnp.bfloat16),
        in_specs=[vmem, vmem, pl.BlockSpec(memory_space=pl.ANY)],
        out_specs=vmem,
        scratch_shapes=[
            pltpu.VMEM((S, S), jnp.float32),
            pltpu.VMEM((S, S), jnp.float32),
            pltpu.VMEM(stacked.shape, jnp.bfloat16),
            pltpu.SemaphoreType.DMA,
        ],
        name="beams",
    )(packed, steer, stacked)


def on_device(voltages, filter_taps, positions, beam_dirs, chan_table):
    snap_count = voltages.shape[2]
    packed, steer, stacked = front(voltages, filter_taps, positions, beam_dirs, chan_table)
    beam_out = beams(
        packed.reshape(S, S), steer, stacked.reshape(2 * S, snap_count), float(snap_count * SEG)
    )
    return beam_out.reshape(1, 2, B, snap_count)


def solution(mesh):
    return jax.shard_map(
        on_device,
        mesh=mesh,
        in_specs=(P("stn", None, "seg"), P(), P(), P(), P()),
        out_specs=P("stn", None, None, "seg"),
        check_vma=False,
    )
```

time: 90.1 us -> 71.3 us (0.79)
  Pallas kernels: 35.2 us -> 65.5 us
  waiting for transfers between devices: 25.7 us -> 0 us
  starting transfers between devices: 13.5 us -> 0 us
  matrix products: 6.29 us -> 0 us
  other arithmetic: 4.04 us -> 0 us
  local copies, waits for them, and re-layouts: 4.23 us -> 5.5 us
    pallas_call x1, Pallas kernels: 16.6 us -> 47.3 us  [front(): pl.pallas_call(front_kernel, out_shape=(jax.ShapeDtypeStruct((SEG, rows,...]
    all_to_all x1 -> x0, waiting for transfers between devices: 25.6 us -> none  [on_device(): lax.all_to_all(spectra, 'stn', split_axis=0, concat_axis=2, tiled=True)]
    all_to_all x1 -> x0, starting transfers between devices: 9.52 us -> none  [on_device(): lax.all_to_all(spectra, 'stn', split_axis=0, concat_axis=2, tiled=True)]
    dot_general x2 -> x0, matrix products: 6.29 us -> none  [the longest x1 5.82 us: channelize(): jnp.einsum('jap,spt->jast', dft_table, filtered, precision=HIGHEST)]
    unnamed x8 -> x16, local copies, waits for them, and re-layouts: 0.02 us -> 5.5 us
    ppermute x1 -> x0, starting transfers between devices: 4.02 us -> none  [passed_along(): return lax.ppermute(value, axis, pairs)]
    convert_element_type x1 -> x0, other arithmetic: 1.6 us -> none  [filter_block(): widened = station_block.astype(jnp.float32)]
    convert_element_type x1 -> x0, local copies, waits for them, and re-layouts: 1.55 us -> none  [channelize(): jnp.einsum('jap,spt->jast', dft_table, filtered, precision=HIGHEST)]
  transfers between devices with their start and end apart: 2 -> 0, of which waited for: 1 -> 0; matrix products, arithmetic and copies ran while one was open for 4% -> 0% of each run, Pallas kernels for 0% -> 0%
where the time goes in v2:
time: 71.3 us; the launch traced here: 71.1 us
  Pallas kernels  65.5 us (92%)
  local copies, waits for them, and re-layouts  5.5 us (8%)
    pallas_call x1, Pallas kernels, front(): pl.pallas_call(front_kernel, out_shape=(jax.ShapeDtypeStruct((SEG, rows,...  47.3 us
    pallas_call x1, Pallas kernels, beams(): pl.pallas_call(functools.partial(beam_kernel, snap_total), out_shape=jax....  18.2 us
    unnamed x16, local copies, waits for them, and re-layouts  5.5 us

profile of v2, /device:TPU:1, one launch (start us, length us, event | category | flops | bytes accessed | tf_op | source)
XLA Modules:
  0.0 71.1 jit_solution(4114004269175645155)
XLA Ops:
  0.0 0.0 copy-start.6
  0.0 0.0 copy-start.5
  0.0 0.7 copy-done.6
  0.7 0.0 copy-done.5
  0.7 0.0 copy-start
  0.7 1.2 %copy-done = bf16[8,32,2048]{2,1,0:T(8,128)(2,1)S(1)} copy-done((bf16[8,32,2048]{2,1,0:T(8,128)(2,1)S(1)}, bf16[8,32,2048]{2,1,0:T(8,128)(2,1)}, u32[]{:S(2)}) %copy-start) | copy-done | bytes 1048600
  1.9 0.0 copy-start.4
  1.9 0.7 copy-done.4
  2.6 0.0 copy-start.7
  2.6 0.7 copy-done.7
  3.3 47.3 %front.1 = (f32[16,8,128]{2,1,0:T(8,128)S(1)}, f32[256,128]{1,0:T(8,128)S(1)}, bf16[2,16,8,2048]{3,2,1,0:T(8,128)(2,1)S(1)}) custom-call(bf16[8,32,2048]{2,1,0:T(8,128)(2,1)S(1)} %copy-done, f32[8,32]{1,0:T(8,128)S(1)} %copy-done.4, f32[2,128]{1,0:T(2,128)S(1)} %copy-done.5, s32[1,128]{1,0:T(1,128)S(1)} %bitcast.6, s32[16]{0:T(128)S(1)} %copy-done.7), custom_call_target="tpu_custom_call" | custom-call | tf_op jit(solution)/shard_map/front/pallas_call | solution.py:215
  50.6 0.0 copy-start.1
  50.6 1.0 %copy-done.1 = bf16[2,16,8,2048]{3,2,1,0:T(8,128)(2,1)} copy-done((bf16[2,16,8,2048]{3,2,1,0:T(8,128)(2,1)}, bf16[2,16,8,2048]{3,2,1,0:T(8,128)(2,1)S(1)}, u32[]{:S(2)}) %copy-start.1) | copy-done | bytes 1048600
  51.6 0.0 copy-start.2
  51.6 0.7 copy-done.2
  52.2 0.0 copy-start.3
  52.2 0.6 copy-done.3
  52.9 18.2 %beams.1 = bf16[256,2048]{1,0:T(8,128)(2,1)} custom-call(f32[128,128]{1,0:T(8,128)} %bitcast.5, f32[256,128]{1,0:T(8,128)} %copy-done.2, bf16[256,2048]{1,0:T(8,128)(2,1)} %bitcast.4), custom_call_target="tpu_custom_call" | custom-call | tf_op jit(solution)/shard_map/beams/pallas_call | solution.py:328
Async XLA Ops:
  0.0 0.7 copy-start.6
  0.0 0.7 copy-start.5
  0.7 1.2 %copy-start = (bf16[8,32,2048]{2,1,0:T(8,128)(2,1)S(1)}, bf16[8,32,2048]{2,1,0:T(8,128)(2,1)}, u32[]{:S(2)}) copy-start(bf16[8,32,2048]{2,1,0:T(8,128)(2,1)} %v_ref.1) | copy-start | bytes 3145732
  1.9 0.7 copy-start.4
  2.6 0.7 copy-start.7
  50.6 1.0 %copy-start.1 = (bf16[2,16,8,2048]{3,2,1,0:T(8,128)(2,1)}, bf16[2,16,8,2048]{3,2,1,0:T(8,128)(2,1)S(1)}, u32[]{:S(2)}) copy-start(bf16[2,16,8,2048]{3,2,1,0:T(8,128)(2,1)S(1)} %get-tuple-element.10) | copy-start | bytes 3145732
  51.6 0.7 copy-start.2
  52.2 0.6 copy-start.3

commit v3 on v2

--- a/solution.py
+++ b/solution.py
@@ -17,6 +17,7 @@
 STN = 16
 CHUNKS = 4
 PAD = 128
+TILE = 512
 
 
 loading_level = 0.1
@@ -25,11 +26,173 @@
 MESH = pl.DeviceIdType.MESH
 
 
+def lane_of(value, i):
+    return jnp.broadcast_to(value[:, i : i + 1], value.shape)
+
+
+def row_of(value, i):
+    return jnp.broadcast_to(value[i : i + 1, :], value.shape)
+
+
+def parts(value):
+    first = value.astype(jnp.bfloat16).astype(jnp.float32)
+    rest = value - first
+    second = rest.astype(jnp.bfloat16).astype(jnp.float32)
+    return first, second, rest - second
+
+
+def eliminate(pr, pi, base, row, lane):
+    cr = [lane_of(pr, base + i) for i in range(8)]
+    ci = [lane_of(pi, base + i) for i in range(8)]
+    for i in range(8):
+        inv = 1.0 / row_of(cr[i], i)
+        here = row == i
+        at = lane == base + i
+        rr = jnp.where(at, inv, row_of(pr, i) * inv)
+        ri = jnp.where(at, 0.0, row_of(pi, i) * inv)
+        nr = jnp.where(at, 0.0, pr) - (cr[i] * rr - ci[i] * ri)
+        ni = jnp.where(at, 0.0, pi) - (cr[i] * ri + ci[i] * rr)
+        pr = jnp.where(here, rr, nr)
+        pi = jnp.where(here, ri, ni)
+        for j in range(i + 1, 8):
+            mr = row_of(cr[j], i) * inv
+            mi = row_of(ci[j], i) * inv
+            nr = cr[j] - (cr[i] * mr - ci[i] * mi)
+            ni = ci[j] - (cr[i] * mi + ci[i] * mr)
+            cr[j] = jnp.where(here, mr, nr)
+            ci[j] = jnp.where(here, mi, ni)
+    return pr, pi
+
+
+def invert_hermitian(hr_ref, hi_ref):
+    count = S // 8
+    lane = lax.broadcasted_iota(jnp.int32, (8, S), 1)
+    row = lax.broadcasted_iota(jnp.int32, (8, S), 0)
+
+    def inside(k):
+        return (lane >= 8 * k) & (lane < 8 * k + 8)
+
+    def load(g):
+        return hr_ref[8 * g : 8 * g + 8, :], hi_ref[8 * g : 8 * g + 8, :]
+
+    def store(g, ar, ai):
+        hr_ref[8 * g : 8 * g + 8, :] = ar
+        hi_ref[8 * g : 8 * g + 8, :] = ai
+
+    def columns(k, panel):
+        pieces = []
+        for value in panel:
+            value = jnp.where(lane < 8 * k, -value, jnp.where(inside(k), 0.0, value))
+            a, b, c = parts(value)
+            pieces += [a, a, b, b, a, c]
+        return jnp.concatenate(pieces, axis=0).astype(jnp.bfloat16)
+
+    def update(cols, panel):
+        ra, rb, rc = parts(panel[0])
+        ia, ib, ic = parts(panel[1])
+        left = [ra, rb, ra, rb, rc, ra, ia, ib, ia, ib, ic, ia]
+        right = [ia, ib, ia, ib, ic, ia, -ra, -rb, -ra, -rb, -rc, -ra]
+        rows = jnp.concatenate(
+            [jnp.concatenate(left, axis=0), jnp.concatenate(right, axis=0)], axis=1
+        ).astype(jnp.bfloat16)
+        return lax.dot_general(
+            cols, rows, (((0,), (0,)), ((), ())), preferred_element_type=jnp.float32
+        )
+
+    def bulk(k, cols, panel, skip):
+        term = update(cols, panel)
+        for g in range(count):
+            if g == k:
+                store(g, *panel)
+            elif g != skip:
+                ar, ai = load(g)
+                ar = jnp.where(inside(k), 0.0, ar) - term[8 * g : 8 * g + 8, :S]
+                ai = jnp.where(inside(k), 0.0, ai) - term[8 * g : 8 * g + 8, S:]
+                store(g, ar, ai)
+
+    panel = load(0)
+    cols = last = None
+    for k in range(count):
+        if k > 0:
+            bulk(k - 1, cols, last, k)
+        cols = columns(k, panel)
+        last = eliminate(*panel, 8 * k, row, lane)
+        if k + 1 < count:
+            hr, hi = load(k + 1)
+            ar = jnp.where(inside(k), 0.0, hr)
+            ai = jnp.where(inside(k), 0.0, hi)
+            for i in range(8):
+                cr, ci = lane_of(hr, 8 * k + i), lane_of(hi, 8 * k + i)
+                rr, ri = row_of(last[0], i), row_of(last[1], i)
+                ar = ar - (cr * rr - ci * ri)
+                ai = ai - (cr * ri + ci * rr)
+            panel = ar, ai
+    bulk(count - 1, cols, last, None)
+
+
+def beam_kernel(snap_total, packed_ref, steer_ref, held_ref, out_ref, hr_ref, hi_ref, beam_ref, sem):
+    packed = packed_ref[...].reshape(S, S)
+    turned = packed.T
+    row = lax.broadcasted_iota(jnp.int32, (S, S), 0)
+    lane = lax.broadcasted_iota(jnp.int32, (S, S), 1)
+    upper, diag = lane > row, lane == row
+    sym = jnp.where(upper, turned, packed) / snap_total
+    skew = jnp.where(upper, packed, -turned) / snap_total
+    hr_ref[...] = sym + jnp.where(diag, loading_level, 0.0)
+    hi_ref[...] = jnp.where(diag, 0.0, skew)
+    invert_hermitian(hr_ref, hi_ref)
+    vr, vi = steer_ref[0:S], steer_ref[S : 2 * S]
+    both = jnp.concatenate([vr, vi], axis=1)
+    by_real = jnp.dot(hr_ref[...], both, precision=HIGHEST, preferred_element_type=jnp.float32)
+    by_imag = jnp.dot(hi_ref[...], both, precision=HIGHEST, preferred_element_type=jnp.float32)
+    wr = by_real[:, :B] - by_imag[:, B:]
+    wi = by_real[:, B:] + by_imag[:, :B]
+    power = jnp.sum(vr * wr + vi * wi, axis=0, keepdims=True)
+    scale = 1.0 / jnp.sqrt(power)
+    wr = (wr * scale).astype(jnp.bfloat16)
+    wi = (wi * scale).astype(jnp.bfloat16)
+    weights = jnp.concatenate([wr, wi], axis=0)
+    swapped = jnp.concatenate([-wi, wr], axis=0)
+    mix = jnp.concatenate([weights, swapped], axis=1).T
+    snaps = out_ref.shape[1]
+    copies = []
+    for n in range(snaps // TILE):
+        at = pl.ds(n * TILE, TILE)
+        block = held_ref[:, :, :, at].reshape(2 * S, TILE)
+        res = jnp.dot(mix, block, preferred_element_type=jnp.float32)
+        beam_ref[:, at] = res.astype(jnp.bfloat16)
+        copy = pltpu.make_async_copy(beam_ref.at[:, at], out_ref.at[:, at], sem.at[n])
+        copy.start()
+        copies.append(copy)
+    for copy in copies:
+        copy.wait()
+
+
+def beams(packed, steer, held, snap_total):
+    vmem = pl.BlockSpec(memory_space=pltpu.VMEM)
+    snaps = held.shape[3]
+    return pl.pallas_call(
+        functools.partial(beam_kernel, snap_total),
+        out_shape=jax.ShapeDtypeStruct((2 * B, snaps), jnp.bfloat16),
+        in_specs=[vmem, vmem, vmem],
+        out_specs=pl.BlockSpec(memory_space=pltpu.HBM),
+        scratch_shapes=[
+            pltpu.VMEM((S, S), jnp.float32),
+            pltpu.VMEM((S, S), jnp.float32),
+            pltpu.VMEM((2 * B, snaps), jnp.bfloat16),
+            pltpu.SemaphoreType.DMA((snaps // TILE,)),
+        ],
+        compiler_params=pltpu.CompilerParams(vmem_limit_bytes=16 * 1024 * 1024),
+        name="beams",
+    )(packed, steer, held)
+
+
 def front_kernel(
-    v_ref, taps_ref, pos_ref, dirs_ref, chan_ref,
-    packed_ref, steer_ref, out_ref,
-    vbuf, spread, spec, land, gram, part, landed,
-    vsem, osem, hsem, send_x, recv_x, send_a, recv_a, send_b, recv_b,
+    v_ref, taps_in, pos_in, dirs_in, chan_in,
+    packed_ref, steer_ref, land,
+    taps_ref, pos_ref, dirs_ref, chan_ref,
+    vbuf, spread, spec, gram, part, landed,
+    asem, vsem, hsem, send_x, recv_x, send_a, recv_a, send_b, recv_b,
 ):
     stn, seg = lax.axis_index("stn"), lax.axis_index("seg")
     stn_peers = [lax.rem(stn + d, STN) for d in range(1, STN)]
@@ -44,6 +207,13 @@
         pl.semaphore_signal(barrier, inc=1, device_id={"stn": peer}, device_id_type=MESH)
     for peer in seg_peers:
         pl.semaphore_signal(barrier, inc=1, device_id={"seg": peer}, device_id_type=MESH)
+    small = []
+    for n, (src, dst) in enumerate(
+        ((chan_in, chan_ref), (taps_in, taps_ref), (pos_in, pos_ref), (dirs_in, dirs_ref))
+    ):
+        fetch = pltpu.make_async_copy(src, dst, asem.at[n])
+        fetch.start()
+        small.append(fetch)
     fetches = []
     for c in range(CHUNKS):
         fetch = pltpu.make_async_copy(
@@ -54,6 +224,8 @@
         fetch.start()
         fetches.append(fetch)
 
+    for fetch in small:
+        fetch.wait()
     row = lax.broadcasted_iota(jnp.int32, (frame, TAPS * frame), 0)
     lane = lax.broadcasted_iota(jnp.int32, (frame, TAPS * frame), 1)
     channel_of = jnp.zeros((frame, TAPS * frame), jnp.int32)
@@ -141,14 +313,10 @@
     steer_ref[0:S, :] = jnp.cos(phases)
     steer_ref[S : 2 * S, :] = jnp.sin(phases)
 
-    stores = []
     for n, c in enumerate(order):
         for copy in sent[c]:
             copy.wait_recv()
         at = pl.ds(c * wide, wide)
-        store = pltpu.make_async_copy(land.at[:, :, :, at], out_ref.at[:, :, :, at], osem.at[c])
-        store.start()
-        stores.append(store)
         block = land[:, :, :, at].reshape(2 * S, wide)
         term = lax.dot_general(
             block, block, (((1,), (1,)), ((), ())), preferred_element_type=jnp.float32
@@ -196,8 +364,6 @@
     for c in order:
         for copy in sent[c]:
             copy.wait_send()
-    for store in stores:
-        store.wait()
     for copy in spread_out:
         copy.wait_send()
     for copy in shared:
@@ -209,8 +375,7 @@
     wide = snaps // CHUNKS
     rows = S // SEG
     vmem = pl.BlockSpec(memory_space=pltpu.VMEM)
-    hbm = pl.BlockSpec(memory_space=pl.ANY)
-    smem = pl.BlockSpec(memory_space=pltpu.SMEM)
+    hbm = pl.BlockSpec(memory_space=pltpu.HBM)
     dma = pltpu.SemaphoreType.DMA
     return pl.pallas_call(
         front_kernel,
@@ -219,17 +384,20 @@
             jax.ShapeDtypeStruct((2 * S, B), jnp.float32),
             jax.ShapeDtypeStruct((2, STN, local, snaps), jnp.bfloat16),
         ),
-        in_specs=[hbm, vmem, vmem, vmem, smem],
-        out_specs=(vmem, vmem, hbm),
+        in_specs=[hbm] * 5,
+        out_specs=(vmem, vmem, vmem),
         scratch_shapes=[
+            pltpu.VMEM(filter_taps.shape, jnp.float32),
+            pltpu.VMEM(positions.shape, jnp.float32),
+            pltpu.VMEM((1, B), jnp.int32),
+            pltpu.SMEM(chan_table.shape, jnp.int32),
             pltpu.VMEM((local, frame, PAD + snaps), jnp.bfloat16),
             pltpu.VMEM((wide // PAD, local * frame, PAD), jnp.float32),
             pltpu.VMEM((CHUNKS, STN, 2, local, wide), jnp.bfloat16),
-            pltpu.VMEM((2, STN, local, snaps), jnp.bfloat16),
             pltpu.VMEM((2 * S, 2 * S), jnp.float32),
             pltpu.VMEM((SEG, rows, S), jnp.float32),
             pltpu.VMEM((SEG - 1, rows, S), jnp.float32),
-            dma((CHUNKS,)),
+            dma((4,)),
             dma((CHUNKS,)),
             dma((2,)),
             dma((CHUNKS, STN - 1)),
@@ -240,112 +408,17 @@
             dma((SEG - 1,)),
         ],
         compiler_params=pltpu.CompilerParams(
-            collective_id=1, has_side_effects=True, vmem_limit_bytes=32 * 1024 * 1024
+            collective_id=1, has_side_effects=True, vmem_limit_bytes=48_000_000
         ),
         name="front",
-    )(voltages, filter_taps, positions, beam_dirs.reshape(1, B), chan_table)
-
-
-def invert_hermitian(hr_ref, hi_ref):
-    groups = S // 8
-    lane = lax.broadcasted_iota(jnp.int32, (8, S), 1)
-    row = lax.broadcasted_iota(jnp.int32, (8, S), 0)
-
-    def trip(_, carry):
-        hr = [hr_ref[pl.ds(8 * g, 8), :] for g in range(groups)]
-        hi = [hi_ref[pl.ds(8 * g, 8), :] for g in range(groups)]
-        pr, pi = hr[0], hi[0]
-        for i in range(8):
-            cr, ci = pr[:, i : i + 1], pi[:, i : i + 1]
-            inv = 1.0 / pr[i : i + 1, i : i + 1]
-            at = lane[0:1] == i
-            rr = jnp.where(at, inv, pr[i : i + 1, :] * inv)
-            ri = jnp.where(at, 0.0, pi[i : i + 1, :] * inv)
-            br = jnp.where(lane == i, 0.0, pr)
-            bi = jnp.where(lane == i, 0.0, pi)
-            nr = br - (cr * rr - ci * ri)
-            ni = bi - (cr * ri + ci * rr)
-            pr = jnp.where(row == i, rr, nr)
-            pi = jnp.where(row == i, ri, ni)
-        for g in range(1, groups):
-            ar = jnp.where(lane < 8, 0.0, hr[g])
-            ai = jnp.where(lane < 8, 0.0, hi[g])
-            for i in range(8):
-                cr, ci = hr[g][:, i : i + 1], hi[g][:, i : i + 1]
-                rr, ri = pr[i : i + 1, :], pi[i : i + 1, :]
-                ar = ar - (cr * rr - ci * ri)
-                ai = ai - (cr * ri + ci * rr)
-            hr_ref[pl.ds(8 * (g - 1), 8), :] = pltpu.roll(ar, S - 8, 1)
-            hi_ref[pl.ds(8 * (g - 1), 8), :] = pltpu.roll(ai, S - 8, 1)
-        hr_ref[pl.ds(S - 8, 8), :] = pltpu.roll(pr, S - 8, 1)
-        hi_ref[pl.ds(S - 8, 8), :] = pltpu.roll(pi, S - 8, 1)
-        return carry
-
-    lax.fori_loop(0, groups, trip, 0)
-
-
-def beam_kernel(snap_total, packed_ref, steer_ref, held_ref, out_ref, hr_ref, hi_ref, stacked_ref, sem):
-    fetch = pltpu.make_async_copy(held_ref, stacked_ref, sem)
-    fetch.start()
-    packed = packed_ref[...]
-    turned = packed.T
-    row = lax.broadcasted_iota(jnp.int32, (S, S), 0)
-    lane = lax.broadcasted_iota(jnp.int32, (S, S), 1)
-    upper = lane > row
-    diag = lane == row
-    sym = jnp.where(upper, turned, packed) / snap_total
-    skew = jnp.where(upper, packed, -turned) / snap_total
-    hr_ref[...] = sym + jnp.where(diag, loading_level, 0.0)
-    hi_ref[...] = jnp.where(diag, 0.0, skew)
-    invert_hermitian(hr_ref, hi_ref)
-    vr, vi = steer_ref[0:S], steer_ref[S : 2 * S]
-    both = jnp.concatenate([vr, vi], axis=1)
-    by_real = jnp.dot(hr_ref[...], both, precision=HIGHEST, preferred_element_type=jnp.float32)
-    by_imag = jnp.dot(hi_ref[...], both, precision=HIGHEST, preferred_element_type=jnp.float32)
-    wr = by_real[:, :B] - by_imag[:, B:]
-    wi = by_real[:, B:] + by_imag[:, :B]
-    power = jnp.sum(vr * wr + vi * wi, axis=0, keepdims=True)
-    scale = 1.0 / jnp.sqrt(power)
-    wr = (wr * scale).astype(jnp.bfloat16)
-    wi = (wi * scale).astype(jnp.bfloat16)
-    weights = jnp.concatenate([wr, wi], axis=0)
-    swapped = jnp.concatenate([-wi, wr], axis=0)
-    mix = jnp.concatenate([weights, swapped], axis=1).T
-    width = 512
-    fetch.wait()
-
-    def tile(n, carry):
-        at = pl.ds(pl.multiple_of(n * width, width), width)
-        res = jnp.dot(mix, stacked_ref[:, at], preferred_element_type=jnp.float32)
-        out_ref[:, at] = res.astype(jnp.bfloat16)
-        return carry
-
-    lax.fori_loop(0, stacked_ref.shape[1] // width, tile, 0)
-
-
-def beams(packed, steer, stacked, snap_total):
-    vmem = pl.BlockSpec(memory_space=pltpu.VMEM)
-    return pl.pallas_call(
-        functools.partial(beam_kernel, snap_total),
-        out_shape=jax.ShapeDtypeStruct((2 * B, stacked.shape[1]), jnp.bfloat16),
-        in_specs=[vmem, vmem, pl.BlockSpec(memory_space=pl.ANY)],
-        out_specs=vmem,
-        scratch_shapes=[
-            pltpu.VMEM((S, S), jnp.float32),
-            pltpu.VMEM((S, S), jnp.float32),
-            pltpu.VMEM(stacked.shape, jnp.bfloat16),
-            pltpu.SemaphoreType.DMA,
-        ],
-        name="beams",
-    )(packed, steer, stacked)
+    )(voltages, filter_taps, positions, beam_dirs, chan_table)
 
 
 def on_device(voltages, filter_taps, positions, beam_dirs, chan_table):
     snap_count = voltages.shape[2]
-    packed, steer, stacked = front(voltages, filter_taps, positions, beam_dirs, chan_table)
-    beam_out = beams(
-        packed.reshape(S, S), steer, stacked.reshape(2 * S, snap_count), float(snap_count * SEG)
-    )
+    stay = lambda x: pltpu.with_memory_space_constraint(x, pltpu.HBM)
+    packed, steer, held = front(stay(voltages), stay(filter_taps), stay(positions), stay(beam_dirs.reshape(1, B)), stay(chan_table))
+    beam_out = beams(packed, steer, held, float(snap_count * SEG))
     return beam_out.reshape(1, 2, B, snap_count)
 
 

time: 71.3 us -> 52.5 us (0.74)
  Pallas kernels: 65.5 us -> 52.4 us
  local copies, waits for them, and re-layouts: 5.5 us -> 0 us
    pallas_call x1, Pallas kernels: 18.2 us -> 5.81 us  [beams(): pl.pallas_call(functools.partial(beam_kernel, snap_total), out_shape=jax....]
    unnamed x16 -> x0, local copies, waits for them, and re-layouts: 5.5 us -> none
where the time goes in v3:
time: 52.5 us
  Pallas kernels  52.4 us (100%)
    pallas_call x1, Pallas kernels, front(): pl.pallas_call(front_kernel, out_shape=(jax.ShapeDtypeStruct((SEG, rows,...  46.6 us
    pallas_call x1, Pallas kernels, beams(): pl.pallas_call(functools.partial(beam_kernel, snap_total), out_shape=jax....  5.81 us

profile of v3, /device:TPU:1, one launch (start us, length us, event | category | flops | bytes accessed | tf_op | source)
XLA Modules:
  0.0 52.5 jit_solution(13813531678385112785)
XLA Ops:
  0.0 46.6 %front.1 = (f32[16,8,128]{2,1,0:T(8,128)S(1)}, f32[256,128]{1,0:T(8,128)S(1)}, bf16[2,16,8,2048]{3,2,1,0:T(8,128)(2,1)S(1)}) custom-call(bf16[8,32,2048]{2,1,0:T(8,128)(2,1)} %v_ref.1, f32[8,32]{1,0:T(8,128)} %taps_in.1, f32[2,128]{1,0:T(2,128)} %pos_in.1, s32[1,128]{1,0:T(1,128)} %bitcast.2, s32[16]{0:T(128)} %chan_in.1), custom_call_target="tpu_custom_call" | custom-call | tf_op jit(solution)/shard_map/front/pallas_call | solution.py:380
  46.6 5.8 %beams.1 = bf16[256,2048]{1,0:T(8,128)(2,1)} custom-call(f32[16,8,128]{2,1,0:T(8,128)S(1)} %get-tuple-element.8.packed_ref, f32[256,128]{1,0:T(8,128)S(1)} %get-tuple-element.9.steer_ref, bf16[2,16,8,2048]{3,2,1,0:T(8,128)(2,1)S(1)} %get-tuple-element.10.held_ref), custom_call_target="tpu_custom_call" | custom-call | tf_op jit(solution)/shard_map/beams/pallas_call | solution.py:174

commit v4 on v3

--- a/solution.py
+++ b/solution.py
@@ -15,9 +15,11 @@
 S = 128
 SEG = 16
 STN = 16
-CHUNKS = 4
+PIECE = 512
+ORDER = ((1536, 512), (512, 1024), (0, 512))
 PAD = 128
 TILE = 512
+SIDE = 4
 
 
 loading_level = 0.1
@@ -130,7 +132,8 @@
     bulk(count - 1, cols, last, None)
 
 
-def beam_kernel(snap_total, packed_ref, steer_ref, held_ref, out_ref, hr_ref, hi_ref, beam_ref, sem):
+def beam_kernel(snap_total, packed_ref, steer_ref, *refs):
+    held, (out_ref, hr_ref, hi_ref, beam_ref, sem) = refs[: len(ORDER)], refs[len(ORDER) :]
     packed = packed_ref[...].reshape(S, S)
     turned = packed.T
     row = lax.broadcasted_iota(jnp.int32, (S, S), 0)
@@ -154,27 +157,30 @@
     weights = jnp.concatenate([wr, wi], axis=0)
     swapped = jnp.concatenate([-wi, wr], axis=0)
     mix = jnp.concatenate([weights, swapped], axis=1).T
-    snaps = out_ref.shape[1]
     copies = []
-    for n in range(snaps // TILE):
-        at = pl.ds(n * TILE, TILE)
-        block = held_ref[:, :, :, at].reshape(2 * S, TILE)
-        res = jnp.dot(mix, block, preferred_element_type=jnp.float32)
-        beam_ref[:, at] = res.astype(jnp.bfloat16)
-        copy = pltpu.make_async_copy(beam_ref.at[:, at], out_ref.at[:, at], sem.at[n])
-        copy.start()
-        copies.append(copy)
+    for ref, (start, wide) in zip(held, ORDER):
+        for n in range(0, wide, TILE):
+            width = min(TILE, wide)
+            res = jnp.dot(
+                mix, stacked(ref, slice(n, n + width)), preferred_element_type=jnp.float32
+            )
+            at = pl.ds(start + n, width)
+            beam_ref[:, at] = res.astype(jnp.bfloat16)
+            copy = pltpu.make_async_copy(
+                beam_ref.at[:, at], out_ref.at[:, at], sem.at[len(copies)]
+            )
+            copy.start()
+            copies.append(copy)
     for copy in copies:
         copy.wait()
 
 
-def beams(packed, steer, held, snap_total):
+def beams(packed, steer, held, snaps):
     vmem = pl.BlockSpec(memory_space=pltpu.VMEM)
-    snaps = held.shape[3]
     return pl.pallas_call(
-        functools.partial(beam_kernel, snap_total),
+        functools.partial(beam_kernel, float(snaps * SEG)),
         out_shape=jax.ShapeDtypeStruct((2 * B, snaps), jnp.bfloat16),
-        in_specs=[vmem, vmem, vmem],
+        in_specs=[vmem] * (2 + len(ORDER)),
         out_specs=pl.BlockSpec(memory_space=pltpu.HBM),
         scratch_shapes=[
             pltpu.VMEM((S, S), jnp.float32),
@@ -184,22 +190,27 @@
         ],
         compiler_params=pltpu.CompilerParams(vmem_limit_bytes=16 * 1024 * 1024),
         name="beams",
-    )(packed, steer, held)
-
-
-def front_kernel(
-    v_ref, taps_in, pos_in, dirs_in, chan_in,
-    packed_ref, steer_ref, land,
-    taps_ref, pos_ref, dirs_ref, chan_ref,
-    vbuf, spread, spec, gram, part, landed,
-    asem, vsem, hsem, send_x, recv_x, send_a, recv_a, send_b, recv_b,
-):
+    )(packed, steer, *held)
+
+
+def stacked(ref, at=slice(None)):
+    both = jnp.concatenate([ref[:, 0, :, at], ref[:, 1, :, at]], axis=0)
+    return both.reshape(2 * S, both.shape[2])
+
+
+def front_kernel(v_ref, taps_in, pos_in, dirs_in, chan_in, packed_ref, steer_ref, *refs):
+    held, refs = refs[: len(ORDER)], refs[len(ORDER) :]
+    specs, refs = refs[: len(ORDER)], refs[len(ORDER) :]
+    (
+        taps_ref, pos_ref, dirs_ref, chan_ref,
+        vbuf, spread, gram, part, landed, middle, landed_b,
+        asem, vsem, hsem, send_x, recv_x, send_a, recv_a,
+    ) = refs
     stn, seg = lax.axis_index("stn"), lax.axis_index("seg")
-    stn_peers = [lax.rem(stn + d, STN) for d in range(1, STN)]
+    stn_peers = [lax.rem(stn + d, STN) for d in (8, 7, 9, 6, 10, 5, 11, 4, 12, 3, 13, 2, 14, 1, 15)]
     seg_peers = [lax.rem(seg + d, SEG) for d in range(1, SEG)]
     local = v_ref.shape[0]
     snaps = v_ref.shape[2]
-    wide = snaps // CHUNKS
     frame = 2 * C
 
     barrier = pltpu.get_barrier_semaphore()
@@ -214,15 +225,17 @@
         fetch = pltpu.make_async_copy(src, dst, asem.at[n])
         fetch.start()
         small.append(fetch)
-    fetches = []
-    for c in range(CHUNKS):
-        fetch = pltpu.make_async_copy(
-            v_ref.at[:, :, pl.ds(c * wide, wide)],
-            vbuf.at[:, :, pl.ds(PAD + c * wide, wide)],
-            vsem.at[c],
-        )
-        fetch.start()
-        fetches.append(fetch)
+    pending = {}
+    for start, wide in ORDER:
+        for n in range((start + wide) // PIECE - 1, max(start - PAD, 0) // PIECE - 1, -1):
+            if n not in pending:
+                fetch = pltpu.make_async_copy(
+                    v_ref.at[:, :, pl.ds(n * PIECE, PIECE)],
+                    vbuf.at[:, :, pl.ds(PAD + n * PIECE, PIECE)],
+                    vsem.at[n],
+                )
+                fetch.start()
+                pending[n] = fetch
 
     for fetch in small:
         fetch.wait()
@@ -241,32 +254,39 @@
     mixed = jnp.concatenate([high, low], axis=0)
 
     def channelize_chunk(c):
+        start, wide = ORDER[c]
+        for n in sorted(pending):
+            if n * PIECE < start + wide and (n + 1) * PIECE > start - PAD:
+                pending.pop(n).wait()
+
         def station(s, carry):
-            x = vbuf[s, :, pl.ds(c * wide, wide + PAD)]
-            moved = [x[:, PAD - m : PAD - m + wide] for m in range(TAPS)]
-            res = jnp.dot(
-                mixed, jnp.concatenate(moved, axis=0), preferred_element_type=jnp.float32
-            )
-            res = res[:frame] + res[frame:]
-            for q in range(wide // PAD):
-                spread[q, pl.ds(pl.multiple_of(s * frame, frame), frame), :] = res[
-                    :, q * PAD : (q + 1) * PAD
-                ]
+            x = vbuf[s, :, pl.ds(start, wide + PAD)]
+            for q in range(0, wide, PIECE):
+                width = min(PIECE, wide)
+                moved = [x[:, PAD - m + q : PAD - m + q + width] for m in range(TAPS)]
+                res = jnp.dot(
+                    mixed, jnp.concatenate(moved, axis=0), preferred_element_type=jnp.float32
+                )
+                res = res[:frame] + res[frame:]
+                for t in range(width // PAD):
+                    spread[q // PAD + t, pl.ds(pl.multiple_of(s * frame, frame), frame), :] = res[
+                        :, t * PAD : (t + 1) * PAD
+                    ]
             return carry
 
         lax.fori_loop(0, local, station, 0, unroll=2)
-        for j in range(C):
-            for a in range(2):
-                for q in range(wide // PAD):
+        for q in range(wide // PAD):
+            for j in range(C):
+                for a in range(2):
                     picked = spread[q, pl.ds(2 * j + a, local, stride=frame), :]
-                    spec[c, j, a, :, q * PAD : (q + 1) * PAD] = picked.astype(jnp.bfloat16)
+                    specs[c][j, a, :, q * PAD : (q + 1) * PAD] = picked.astype(jnp.bfloat16)
 
     def send_chunk(c):
         copies = []
         for d, peer in enumerate(stn_peers):
             copy = pltpu.make_async_remote_copy(
-                src_ref=spec.at[c, peer],
-                dst_ref=land.at[:, stn, :, pl.ds(c * wide, wide)],
+                src_ref=specs[c].at[peer],
+                dst_ref=held[c].at[stn],
                 send_sem=send_x.at[c, d],
                 recv_sem=recv_x.at[c, d],
                 device_id={"stn": peer},
@@ -274,28 +294,23 @@
             )
             copy.start()
             copies.append(copy)
-        land[:, stn, :, pl.ds(c * wide, wide)] = spec[c, stn]
+        held[c][stn] = specs[c][stn]
         return copies
 
-    order = list(range(1, CHUNKS)) + [0]
-    for c in range(2):
-        fetches[c].wait()
-    channelize_chunk(order[0])
+    channelize_chunk(0)
     pl.semaphore_wait(barrier, STN - 1 + SEG - 1)
     halo = pltpu.make_async_remote_copy(
         src_ref=v_ref.at[:, :, pl.ds(snaps - PAD, PAD)],
         dst_ref=vbuf.at[:, :, pl.ds(0, PAD)],
         send_sem=hsem.at[0],
         recv_sem=hsem.at[1],
-        device_id={"seg": seg_peers[0]},
+        device_id={"seg": lax.rem(seg + 1, SEG)},
         device_id_type=MESH,
     )
     halo.start()
-    sent = {order[0]: send_chunk(order[0])}
-    for c in order[1:]:
-        if c >= 2:
-            fetches[c].wait()
-        if c == 0:
+    sent = [send_chunk(0)]
+    for c in range(1, len(ORDER)):
+        if ORDER[c][0] == 0:
             halo.wait()
 
             @pl.when(seg == 0)
@@ -303,7 +318,7 @@
                 vbuf[:, :, 0:PAD] = jnp.zeros((local, frame, PAD), jnp.bfloat16)
 
         channelize_chunk(c)
-        sent[c] = send_chunk(c)
+        sent.append(send_chunk(c))
 
     bearing = dirs_ref[...].astype(jnp.float32) * (full_turn / DIRS)
     frequency = 1.0 + chan_ref[stn].astype(jnp.float32) / C
@@ -313,11 +328,10 @@
     steer_ref[0:S, :] = jnp.cos(phases)
     steer_ref[S : 2 * S, :] = jnp.sin(phases)
 
-    for n, c in enumerate(order):
-        for copy in sent[c]:
+    for n, copies in enumerate(sent):
+        for copy in copies:
             copy.wait_recv()
-        at = pl.ds(c * wide, wide)
-        block = land[:, :, :, at].reshape(2 * S, wide)
+        block = stacked(held[n])
         term = lax.dot_general(
             block, block, (((1,), (1,)), ((), ())), preferred_element_type=jnp.float32
         )
@@ -332,47 +346,48 @@
     lane = lax.broadcasted_iota(jnp.int32, (S, S), 1)
     part[...] = jnp.where(lane > row, skew, sym).reshape(part.shape)
 
-    spread_out = []
-    for d, peer in enumerate(seg_peers):
-        copy = pltpu.make_async_remote_copy(
-            src_ref=part.at[peer],
-            dst_ref=landed.at[d],
-            send_sem=send_a.at[d],
-            recv_sem=recv_a.at[d],
-            device_id={"seg": peer},
-            device_id_type=MESH,
-        )
-        copy.start()
-        spread_out.append(copy)
-    total = part[seg]
-    for d, copy in enumerate(spread_out):
-        copy.wait_recv()
-        total = total + landed[d]
-    packed_ref[seg] = total
-    shared = []
-    for d, peer in enumerate(seg_peers):
-        copy = pltpu.make_async_remote_copy(
-            src_ref=packed_ref.at[seg],
-            dst_ref=packed_ref.at[seg],
-            send_sem=send_b.at[d],
-            recv_sem=recv_b.at[d],
-            device_id={"seg": peer},
-            device_id_type=MESH,
-        )
-        copy.start()
-        shared.append(copy)
-    for c in order:
-        for copy in sent[c]:
+    across = [lax.rem(seg // SIDE + d, SIDE) * SIDE + lax.rem(seg, SIDE) for d in (2, 1, 3)]
+    along = [seg // SIDE * SIDE + lax.rem(seg + d, SIDE) for d in (2, 1, 3)]
+    half = SEG // 2
+
+    def exchange(source, target, ways, n):
+        copies = []
+        for d in range(SIDE - 1):
+            for h in range(2):
+                copy = pltpu.make_async_remote_copy(
+                    src_ref=source.at[pl.ds(h * half, half)],
+                    dst_ref=target.at[d, pl.ds(h * half, half)],
+                    send_sem=send_a.at[n, d, h],
+                    recv_sem=recv_a.at[n, d, h],
+                    device_id={"seg": ways[h][d]},
+                    device_id_type=MESH,
+                )
+                copy.start()
+                copies.append(copy)
+        return copies
+
+    first = exchange(part, landed, (along, across), 0)
+    for h in range(2):
+        for copy in first[h::2]:
+            copy.wait_recv()
+        at = pl.ds(h * half, half)
+        middle[at] = part[at] + landed[0, at] + landed[1, at] + landed[2, at]
+    second = exchange(middle, landed_b, (across, along), 1)
+    for h in range(2):
+        for copy in second[h::2]:
+            copy.wait_recv()
+        at = pl.ds(h * half, half)
+        packed_ref[at] = middle[at] + landed_b[0, at] + landed_b[1, at] + landed_b[2, at]
+    for copies in sent:
+        for copy in copies:
             copy.wait_send()
-    for copy in spread_out:
+    for copy in first + second:
         copy.wait_send()
-    for copy in shared:
-        copy.wait()
 
 
 def front(voltages, filter_taps, positions, beam_dirs, chan_table):
     local, frame, snaps = voltages.shape
-    wide = snaps // CHUNKS
+    widths = [wide for _, wide in ORDER]
     rows = S // SEG
     vmem = pl.BlockSpec(memory_space=pltpu.VMEM)
     hbm = pl.BlockSpec(memory_space=pltpu.HBM)
@@ -382,30 +397,30 @@
         out_shape=(
             jax.ShapeDtypeStruct((SEG, rows, S), jnp.float32),
             jax.ShapeDtypeStruct((2 * S, B), jnp.float32),
-            jax.ShapeDtypeStruct((2, STN, local, snaps), jnp.bfloat16),
+            *[jax.ShapeDtypeStruct((STN, 2, local, wide), jnp.bfloat16) for wide in widths],
         ),
         in_specs=[hbm] * 5,
-        out_specs=(vmem, vmem, vmem),
+        out_specs=(vmem,) * (2 + len(ORDER)),
         scratch_shapes=[
+            *[pltpu.VMEM((STN, 2, local, wide), jnp.bfloat16) for wide in widths],
             pltpu.VMEM(filter_taps.shape, jnp.float32),
             pltpu.VMEM(positions.shape, jnp.float32),
             pltpu.VMEM((1, B), jnp.int32),
             pltpu.SMEM(chan_table.shape, jnp.int32),
             pltpu.VMEM((local, frame, PAD + snaps), jnp.bfloat16),
-            pltpu.VMEM((wide // PAD, local * frame, PAD), jnp.float32),
-            pltpu.VMEM((CHUNKS, STN, 2, local, wide), jnp.bfloat16),
+            pltpu.VMEM((max(widths) // PAD, local * frame, PAD), jnp.float32),
             pltpu.VMEM((2 * S, 2 * S), jnp.float32),
             pltpu.VMEM((SEG, rows, S), jnp.float32),
-            pltpu.VMEM((SEG - 1, rows, S), jnp.float32),
+            pltpu.VMEM((SIDE - 1, SEG, rows, S), jnp.float32),
+            pltpu.VMEM((SEG, rows, S), jnp.float32),
+            pltpu.VMEM((SIDE - 1, SEG, rows, S), jnp.float32),
             dma((4,)),
-            dma((CHUNKS,)),
+            dma((snaps // PIECE,)),
             dma((2,)),
-            dma((CHUNKS, STN - 1)),
-            dma((CHUNKS, STN - 1)),
-            dma((SEG - 1,)),
-            dma((SEG - 1,)),
-            dma((SEG - 1,)),
-            dma((SEG - 1,)),
+            dma((len(ORDER), STN - 1)),
+            dma((len(ORDER), STN - 1)),
+            dma((2, SIDE - 1, 2)),
+            dma((2, SIDE - 1, 2)),
         ],
         compiler_params=pltpu.CompilerParams(
             collective_id=1, has_side_effects=True, vmem_limit_bytes=48_000_000
@@ -417,8 +432,8 @@
 def on_device(voltages, filter_taps, positions, beam_dirs, chan_table):
     snap_count = voltages.shape[2]
     stay = lambda x: pltpu.with_memory_space_constraint(x, pltpu.HBM)
-    packed, steer, held = front(stay(voltages), stay(filter_taps), stay(positions), stay(beam_dirs.reshape(1, B)), stay(chan_table))
-    beam_out = beams(packed, steer, held, float(snap_count * SEG))
+    packed, steer, *held = front(stay(voltages), stay(filter_taps), stay(positions), stay(beam_dirs.reshape(1, B)), stay(chan_table))
+    beam_out = beams(packed, steer, held, snap_count)
     return beam_out.reshape(1, 2, B, snap_count)
 
 

time: 52.5 us -> 49.2 us (0.937)
  Pallas kernels: 52.4 us -> 49.1 us
    pallas_call x1, Pallas kernels: 46.6 us -> 43.3 us  [front(): pl.pallas_call(front_kernel, out_shape=(jax.ShapeDtypeStruct((SEG, rows,...]
where the time goes in v4:
time: 49.2 us; the launch traced here: 49.1 us
  Pallas kernels  49.1 us (100%)
    pallas_call x1, Pallas kernels, front(): pl.pallas_call(front_kernel, out_shape=(jax.ShapeDtypeStruct((SEG, rows,...  43.3 us
    pallas_call x1, Pallas kernels, beams(): pl.pallas_call(functools.partial(beam_kernel, float(snaps * SEG)), out_sh...  5.81 us

profile of v4, /device:TPU:1, one launch (start us, length us, event | category | flops | bytes accessed | tf_op | source)
XLA Modules:
  0.0 49.1 jit_solution(17096096841227419727)
XLA Ops:
  0.0 43.3 %front.1 = (f32[16,8,128]{2,1,0:T(8,128)S(1)}, f32[256,128]{1,0:T(8,128)S(1)}, bf16[16,2,8,512]{3,2,1,0:T(8,128)(2,1)S(1)}, bf16[16,2,8,1024]{3,2,1,0:T(8,128)(2,1)S(1)}, bf16[16,2,8,512]{3,2,1,0:T(8,128)(2,1)S(1)}) custom-call(bf16[8,32,2048]{2,1,0:T(8,128)(2,1)} %v_ref.1, f32[8,32]{1,0:T(8,128)} %taps_in.1, f32[2,128]{1,0:T(2,128)} %pos_in.1, ...), custom_call_target="tpu_custom_call" | custom-call | tf_op jit(solution)/shard_map/front/pallas_call | solution.py:395
  43.3 5.8 %beams.1 = bf16[256,2048]{1,0:T(8,128)(2,1)} custom-call(f32[16,8,128]{2,1,0:T(8,128)S(1)} %get-tuple-element.10.packed_ref, f32[256,128]{1,0:T(8,128)S(1)} %get-tuple-element.11.steer_ref, bf16[16,2,8,512]{3,2,1,0:T(8,128)(2,1)S(1)} %get-tuple-element.12.refs_0_, bf16[16,2,8,1024]{3,2,1,0:T(8,128)(2,1)S(1)} %get-tuple-element.13.refs_1_, ...), custom_call_target="tpu_custom_call" | custom-call | tf_op jit(solution)/shard_map/beams/pallas_call | solution.py:180

commit v5 on v4

--- a/solution.py
+++ b/solution.py
@@ -46,24 +46,47 @@
 def eliminate(pr, pi, base, row, lane):
     cr = [lane_of(pr, base + i) for i in range(8)]
     ci = [lane_of(pi, base + i) for i in range(8)]
+    pivot = row_of(cr[0], 0)
     for i in range(8):
-        inv = 1.0 / row_of(cr[i], i)
+        inv = 1.0 / pivot
+        if i < 7:
+            br, bi = row_of(cr[i + 1], i), row_of(ci[i + 1], i)
+            pivot = row_of(cr[i + 1], i + 1) - (br * br + bi * bi) * inv
         here = row == i
+        gr = jnp.where(here, -1.0, cr[i]) * inv
+        gi = jnp.where(here, 0.0, ci[i]) * inv
+        for j in range(i + 1, 8):
+            br, bi = row_of(cr[j], i), row_of(ci[j], i)
+            cr[j] = jnp.where(here, 0.0, cr[j]) - (gr * br - gi * bi)
+            ci[j] = jnp.where(here, 0.0, ci[j]) - (gr * bi + gi * br)
         at = lane == base + i
-        rr = jnp.where(at, inv, row_of(pr, i) * inv)
-        ri = jnp.where(at, 0.0, row_of(pi, i) * inv)
-        nr = jnp.where(at, 0.0, pr) - (cr[i] * rr - ci[i] * ri)
-        ni = jnp.where(at, 0.0, pi) - (cr[i] * ri + ci[i] * rr)
-        pr = jnp.where(here, rr, nr)
-        pi = jnp.where(here, ri, ni)
-        for j in range(i + 1, 8):
-            mr = row_of(cr[j], i) * inv
-            mi = row_of(ci[j], i) * inv
-            nr = cr[j] - (cr[i] * mr - ci[i] * mi)
-            ni = ci[j] - (cr[i] * mi + ci[i] * mr)
-            cr[j] = jnp.where(here, mr, nr)
-            ci[j] = jnp.where(here, mi, ni)
+        br = jnp.where(at, 1.0, row_of(pr, i))
+        bi = jnp.where(at, 0.0, row_of(pi, i))
+        cross = here | at
+        pr = jnp.where(cross, 0.0, pr) - (gr * br - gi * bi)
+        pi = jnp.where(cross, 0.0, pi) - (gr * bi + gi * br)
     return pr, pi
+
+
+def tree_sum(terms):
+    while len(terms) > 1:
+        terms = [a + b for a, b in zip(terms[::2], terms[1::2])]
+    return terms[0]
+
+
+def subtract_block(group, base, panel, lane):
+    hr, hi = group
+    inside = (lane >= base) & (lane < base + 8)
+    real, imag = [], []
+    for i in range(8):
+        cr, ci = lane_of(hr, base + i), lane_of(hi, base + i)
+        rr, ri = row_of(panel[0], i), row_of(panel[1], i)
+        real.append(cr * rr - ci * ri)
+        imag.append(cr * ri + ci * rr)
+    return (
+        jnp.where(inside, 0.0, hr) - tree_sum(real),
+        jnp.where(inside, 0.0, hi) - tree_sum(imag),
+    )
 
 
 def invert_hermitian(hr_ref, hi_ref):
@@ -106,7 +129,7 @@
         for g in range(count):
             if g == k:
                 store(g, *panel)
-            elif g != skip:
+            elif g not in skip:
                 ar, ai = load(g)
                 ar = jnp.where(inside(k), 0.0, ar) - term[8 * g : 8 * g + 8, :S]
                 ai = jnp.where(inside(k), 0.0, ai) - term[8 * g : 8 * g + 8, S:]
@@ -116,20 +139,13 @@
     cols = last = None
     for k in range(count):
         if k > 0:
-            bulk(k - 1, cols, last, k)
+            bulk(k - 1, cols, last, (k,))
+        ahead = load(k + 1) if k + 1 < count else None
         cols = columns(k, panel)
         last = eliminate(*panel, 8 * k, row, lane)
-        if k + 1 < count:
-            hr, hi = load(k + 1)
-            ar = jnp.where(inside(k), 0.0, hr)
-            ai = jnp.where(inside(k), 0.0, hi)
-            for i in range(8):
-                cr, ci = lane_of(hr, 8 * k + i), lane_of(hi, 8 * k + i)
-                rr, ri = row_of(last[0], i), row_of(last[1], i)
-                ar = ar - (cr * rr - ci * ri)
-                ai = ai - (cr * ri + ci * rr)
-            panel = ar, ai
-    bulk(count - 1, cols, last, None)
+        if ahead is not None:
+            panel = subtract_block(ahead, 8 * k, last, lane)
+    bulk(count - 1, cols, last, ())
 
 
 def beam_kernel(snap_total, packed_ref, steer_ref, *refs):

time: 49.2 us -> 49 us (level)
  no operation moved by 1% of the time
where the time goes in v5:
time: 49 us; the launch traced here: 48.9 us
  Pallas kernels  48.9 us (100%)
    pallas_call x1, Pallas kernels, front(): pl.pallas_call(front_kernel, out_shape=(jax.ShapeDtypeStruct((SEG, rows,...  43.3 us
    pallas_call x1, Pallas kernels, beams(): pl.pallas_call(functools.partial(beam_kernel, float(snaps * SEG)), out_sh...  5.61 us

profile of v5, /device:TPU:1, one launch (start us, length us, event | category | flops | bytes accessed | tf_op | source)
XLA Modules:
  0.0 48.9 jit_solution(17912110759696618364)
XLA Ops:
  0.0 43.3 %front.1 = (f32[16,8,128]{2,1,0:T(8,128)S(1)}, f32[256,128]{1,0:T(8,128)S(1)}, bf16[16,2,8,512]{3,2,1,0:T(8,128)(2,1)S(1)}, bf16[16,2,8,1024]{3,2,1,0:T(8,128)(2,1)S(1)}, bf16[16,2,8,512]{3,2,1,0:T(8,128)(2,1)S(1)}) custom-call(bf16[8,32,2048]{2,1,0:T(8,128)(2,1)} %v_ref.1, f32[8,32]{1,0:T(8,128)} %taps_in.1, f32[2,128]{1,0:T(2,128)} %pos_in.1, ...), custom_call_target="tpu_custom_call" | custom-call | tf_op jit(solution)/shard_map/front/pallas_call | solution.py:411
  43.3 5.6 %beams.1 = bf16[256,2048]{1,0:T(8,128)(2,1)} custom-call(f32[16,8,128]{2,1,0:T(8,128)S(1)} %get-tuple-element.10.packed_ref, f32[256,128]{1,0:T(8,128)S(1)} %get-tuple-element.11.steer_ref, bf16[16,2,8,512]{3,2,1,0:T(8,128)(2,1)S(1)} %get-tuple-element.12.refs_0_, bf16[16,2,8,1024]{3,2,1,0:T(8,128)(2,1)S(1)} %get-tuple-element.13.refs_1_, ...), custom_call_target="tpu_custom_call" | custom-call | tf_op jit(solution)/shard_map/beams/pallas_call | solution.py:196
